TPU v7x, 512 devices: a whole 4x8x8 slice. The times are simulated.
512 devices in a mesh: group: 16 (over x_lo, z), space: 32 (over x_hi, y, core).
Axes of the slice: x: 4 (x_hi: 2, x_lo: 2; x = x_hi * 2 + x_lo), y: 8, z: 8, core: 2. Of those that a mesh axis runs over, the one named last changes fastest.
Arguments:
- pressure: float32 [1024, 512, 128], P('space', 'group'), may hold values from -6 to 6
- source: float32 [1024, 512, 128], P('space', 'group'), may hold values from -4 to 4
- labels: int32 [1024, 512], P('space', 'group'), may hold values from 0 to 15
- region_table: float32 [16, 128], replicated, may hold values from 0.05 to 2
Outputs:
- residual: float32 [1024, 512, 128], P('space', 'group')
- correction: float32 [1024, 512, 128], P('space', 'group')
All inputs are finite; a program needn't handle non-finite values.
Results may differ from a plain program's by a relative error of at most 0.00013.
Values sent between devices are 32-bit elements; how exact they have to be, the bound alone decides.
A program may use at most 64 MiB of HBM per device.

v0:
```python
import math

import jax
import jax.numpy as jnp
from jax import lax
from jax.sharding import PartitionSpec as P

SWEEPS = 4


relax_weight = 0.8
centre_weight = 0.5
side_weight = 0.125


def padded_2(cells, sides, width):
    for axis, dim in sides:
        count = lax.axis_size(axis)
        ends = count - 1
        head = lax.slice_in_dim(cells, 0, width, axis=dim)
        tail = lax.slice_in_dim(cells, cells.shape[dim] - width, cells.shape[dim], axis=dim)
        cells = jnp.concatenate(
            [
                lax.ppermute(tail, axis, [(i, (i + 1) % count) for i in range(ends)]),
                cells,
                lax.ppermute(head, axis, [((i + 1) % count, i) for i in range(ends)]),
            ],
            axis=dim,
        )
    return cells


def face_weights(coeff_pad, scale):
    rows = coeff_pad.shape[0] - 2
    cols = coeff_pad.shape[1] - 2
    centre = coeff_pad[1:-1, 1:-1]
    depth = centre.shape[2]
    faces = []
    for shift_x, shift_y in ((2, 1), (0, 1), (1, 2), (1, 0)):
        nearby = coeff_pad[shift_x : shift_x + rows, shift_y : shift_y + cols]
        faces.append(scale * 0.5 * (centre + nearby))
    column = jnp.pad(centre, ((0, 0), (0, 0), (1, 1)))
    for shift_z in (2, 0):
        faces.append(0.5 * (centre + column[:, :, shift_z : shift_z + depth]))
    diagonal = faces[0]
    for face in faces[1:]:
        diagonal = diagonal + face
    return (faces, diagonal)


def apply_faces(field_pad, faces):
    rows = field_pad.shape[0] - 2
    cols = field_pad.shape[1] - 2
    centre = field_pad[1:-1, 1:-1]
    depth = centre.shape[2]
    column = jnp.pad(centre, ((0, 0), (0, 0), (1, 1)))
    nearby = [
        field_pad[sx : sx + rows, sy : sy + cols] for sx, sy in ((2, 1), (0, 1), (1, 2), (1, 0))
    ]
    nearby = nearby + [column[:, :, sz : sz + depth] for sz in (2, 0)]
    total = faces[0] * (centre - nearby[0])
    for index in range(1, 6):
        total = total + faces[index] * (centre - nearby[index])
    return total


def blend(padded):
    centre = padded[1:-1, 1:-1]
    sides = padded[2:, 1:-1] + padded[:-2, 1:-1]
    sides = sides + padded[1:-1, 2:]
    sides = sides + padded[1:-1, :-2]
    return centre_weight * centre + side_weight * sides


def pad_columns(field):
    return jnp.pad(field, ((0, 0), (1, 1), (0, 0)))


def lookup(tags, table):
    count = table.shape[0]
    onehot = (tags[..., None] == jnp.arange(count, dtype=jnp.int32)).astype(jnp.float32)
    values = jnp.dot(
        onehot.reshape(-1, count),
        table,
        precision=lax.Precision.HIGHEST,
        preferred_element_type=jnp.float32,
    )
    return values.reshape(tags.shape + (table.shape[1],))


def split_grid(field, factor):
    rows, cols, depth = field.shape
    crow = rows // factor
    ccol = cols // factor
    return (
        field.reshape(crow, factor, ccol, factor, depth)
        .transpose(1, 3, 0, 2, 4)
        .reshape(factor * factor, crow, ccol, depth)
    )


def per_device(pressure, source, labels, region_table):
    factor = math.isqrt(lax.axis_size("group"))
    rows, cols, depth = pressure.shape
    crow = rows // factor
    ccol = cols // factor
    scale = 1.0
    coeff = lookup(labels, region_table)
    paired = padded_2(jnp.stack([pressure, coeff]), (("group", 2), ("space", 1)), 1)
    faces, _ = face_weights(paired[1], 1.0)
    residual = source - apply_faces(paired[0], faces)
    widened = padded_2(residual, (("group", 1), ("space", 0)), 1)
    restricted = blend(widened)
    packed = jnp.stack([split_grid(restricted, factor), split_grid(coeff, factor)])
    moved = lax.all_to_all(packed, "group", split_axis=1, concat_axis=3, tiled=True)
    rhs = moved[0, 0]
    coarse_coeff = moved[1, 0]
    coeff_rows = padded_2(coarse_coeff, (("space", 0),), 1)
    coarse_faces, diagonal = face_weights(pad_columns(coeff_rows), scale)
    iterate = relax_weight * rhs / diagonal
    for sweep in range(SWEEPS - 1):
        iterate_rows = padded_2(iterate, (("space", 0),), 1)
        iterate = (
            iterate
            + relax_weight * (rhs - apply_faces(pad_columns(iterate_rows), coarse_faces)) / diagonal
        )
    back = lax.all_to_all(iterate[None], "group", split_axis=2, concat_axis=0, tiled=True)
    spread = (
        back.reshape(factor, factor, crow, ccol, depth)
        .transpose(2, 0, 3, 1, 4)
        .reshape(rows, cols, depth)
    )
    widened_spread = padded_2(spread, (("group", 1), ("space", 0)), 1)
    correction = blend(widened_spread)
    return (residual, correction)


def solution(mesh):
    placed = (P("space", "group", None), P("space", "group", None), P("space", "group"), P())
    return jax.shard_map(
        per_device,
        mesh=mesh,
        in_specs=placed,
        out_specs=(P("space", "group", None), P("space", "group", None)),
        check_vma=False,
    )
```

profile of v0, /device:TPU:6, one launch (start us, length us, event | category | flops | bytes accessed | tf_op | source)
XLA Modules:
  0.0 176.7 jit_solution(10005263130704173237)
XLA Ops:
  0.6 0.0 copy-start
  0.6 0.0 copy-start.2
  0.7 0.8 eq.16
  1.5 0.5 fusion.101
  2.0 1.0 pad_maximum_fusion.31
  3.0 4.3 %collective-permute-start = (f32[2,32,1,128]{3,2,1,0:T(1,128)S(1)}, f32[2,32,1,128]{3,2,1,0:T(1,128)S(1)}, u32[]{:S(2)}, u32[]{:S(2)}) collective-permute-start(f32[2,32,1,128]{3,2,1,0:T(1,128)S(1)} %get-tuple-element.13), channel_id=1, source_target_pairs={{0,32},{32,64},{64,96},{96,128},{128,160},{160,192},{192,224},{224... | collective-permute-start | bytes 98312 | tf_op jit(solution)/shard_map/ppermute | solution.py:24
  7.3 8.9 %collective-permute-start.1 = (f32[2,32,1,128]{3,2,1,0:T(1,128)S(1)}, f32[2,32,1,128]{3,2,1,0:T(1,128)S(1)}, u32[]{:S(2)}, u32[]{:S(2)}) collective-permute-start(f32[2,32,1,128]{3,2,1,0:T(1,128)S(1)} %get-tuple-element.14), channel_id=1, source_target_pairs={{32,0},{64,32},{96,64},{128,96},{160,128},{192,160},{224,192},{256... | collective-permute-start | bytes 98312 | tf_op jit(solution)/shard_map/ppermute | solution.py:26
  16.1 0.0 collective-permute-done
  16.2 1.6 collective-permute-done.1
  17.7 1.9 %collective-permute-start.2 = (f32[2,1,34,128]{3,2,1,0:T(8,128)S(1)}, f32[2,1,34,128]{3,2,1,0:T(8,128)S(1)}, u32[]{:S(2)}, u32[]{:S(2)}) collective-permute-start(f32[2,1,34,128]{3,2,1,0:T(8,128)S(1)} %get-tuple-element.9), channel_id=1, source_target_pairs={{0,1},{1,2},{2,3},{3,4},{4,5},{5,6},{6,7},{7,8},{8,9},{9,10},{10,1... | collective-permute-start | bytes 104456 | tf_op jit(solution)/shard_map/ppermute | solution.py:24
  19.7 7.3 %collective-permute-start.3 = (f32[2,1,34,128]{3,2,1,0:T(8,128)S(1)}, f32[2,1,34,128]{3,2,1,0:T(8,128)S(1)}, u32[]{:S(2)}, u32[]{:S(2)}) collective-permute-start(f32[2,1,34,128]{3,2,1,0:T(8,128)S(1)} %get-tuple-element.10), channel_id=1, source_target_pairs={{1,0},{2,1},{3,2},{4,3},{5,4},{6,5},{7,6},{8,7},{9,8},{10,9},{11,1... | collective-permute-start | bytes 104456 | tf_op jit(solution)/shard_map/ppermute | solution.py:26
  26.9 1.6 collective-permute-done.3
  28.6 0.2 pad_maximum_fusion
  28.8 0.1 slice_bitcast_fusion
  28.9 0.0 copy-start.3
  28.9 0.1 slice.328
  29.0 0.1 slice.325
  29.0 0.9 copy-done.3
  29.9 0.8 fusion.6
  30.7 0.0 copy-start.1
  30.8 6.3 %collective-permute-start.5 = (f32[32,1,128]{2,1,0:T(1,128)S(1)}, f32[32,1,128]{2,1,0:T(1,128)S(1)}, u32[]{:S(2)}, u32[]{:S(2)}) collective-permute-start(f32[32,1,128]{2,1,0:T(1,128)S(1)} %get-tuple-element.27), channel_id=1, source_target_pairs={{32,0},{64,32},{96,64},{128,96},{160,128},{192,160},{224,192},{256... | collective-permute-start | bytes 49160 | tf_op jit(solution)/shard_map/ppermute | solution.py:26
  37.1 1.9 %collective-permute-start.4 = (f32[32,1,128]{2,1,0:T(1,128)S(1)}, f32[32,1,128]{2,1,0:T(1,128)S(1)}, u32[]{:S(2)}, u32[]{:S(2)}) collective-permute-start(f32[32,1,128]{2,1,0:T(1,128)S(1)} %get-tuple-element.28), channel_id=1, source_target_pairs={{0,32},{32,64},{64,96},{96,128},{128,160},{160,192},{192,224},{224... | collective-permute-start | bytes 49160 | tf_op jit(solution)/shard_map/ppermute | solution.py:24
  39.0 5.8 %collective-permute-done.4 = f32[32,1,128]{2,1,0:T(1,128)S(1)} collective-permute-done((f32[32,1,128]{2,1,0:T(1,128)S(1)}, f32[32,1,128]{2,1,0:T(1,128)S(1)}, u32[]{:S(2)}, u32[]{:S(2)}) %collective-permute-start.4) | collective-permute-done | bytes 16416 | tf_op jit(solution)/shard_map/ppermute | solution.py:24
  44.8 6.5 %collective-permute-start.6 = (f32[1,34,128]{2,1,0:T(8,128)S(1)}, f32[1,34,128]{2,1,0:T(8,128)S(1)}, u32[]{:S(2)}, u32[]{:S(2)}) collective-permute-start(f32[1,34,128]{2,1,0:T(8,128)S(1)} %get-tuple-element.17), channel_id=1, source_target_pairs={{1,0},{2,1},{3,2},{4,3},{5,4},{6,5},{7,6},{8,7},{9,8},{10,9},{11,1... | collective-permute-start | bytes 52232 | tf_op jit(solution)/shard_map/ppermute | solution.py:26
  51.3 1.9 %collective-permute-start.7 = (f32[1,34,128]{2,1,0:T(8,128)S(1)}, f32[1,34,128]{2,1,0:T(8,128)S(1)}, u32[]{:S(2)}, u32[]{:S(2)}) collective-permute-start(f32[1,34,128]{2,1,0:T(8,128)S(1)} %get-tuple-element.18), channel_id=1, source_target_pairs={{0,1},{1,2},{2,3},{3,4},{4,5},{5,6},{6,7},{7,8},{8,9},{9,10},{10,1... | collective-permute-start | bytes 52232 | tf_op jit(solution)/shard_map/ppermute | solution.py:24
  53.3 6.8 %collective-permute-done.7 = f32[1,34,128]{2,1,0:T(8,128)S(1)} collective-permute-done((f32[1,34,128]{2,1,0:T(8,128)S(1)}, f32[1,34,128]{2,1,0:T(8,128)S(1)}, u32[]{:S(2)}, u32[]{:S(2)}) %collective-permute-start.7) | collective-permute-done | bytes 17440 | tf_op jit(solution)/shard_map/ppermute | solution.py:24
  60.1 0.2 fusion.86
  60.4 0.1 pad_maximum_fusion.1
  60.5 0.1 copy.24
  60.6 23.4 %all_to_all.30 = f32[2,16,8,8,128]{4,3,2,0,1:T(8,128)S(1)} all-to-all(f32[2,16,8,8,128]{4,3,2,0,1:T(8,128)S(1)} %copy.24), channel_id=1, replica_groups=mesh['group'=16,'space'=32] {'group'}, dimensions={1} | all-to-all | bytes 2097152 | tf_op jit(solution)/shard_map/all_to_all | solution.py:115
  84.0 0.1 copy.33
  84.2 1.9 %collective-permute-start.9 = (f32[1,128,128]{2,1,0:T(8,128)S(1)}, f32[1,128,128]{2,1,0:T(8,128)S(1)}, u32[]{:S(2)}, u32[]{:S(2)}) collective-permute-start(f32[1,128,128]{2,1,0:T(8,128)S(1)} %get-tuple-element.11), channel_id=1, source_target_pairs={{0,1},{1,2},{2,3},{3,4},{4,5},{5,6},{6,7},{7,8},{8,9},{9,10},{10,1... | collective-permute-start | bytes 196616 | tf_op jit(solution)/shard_map/ppermute | solution.py:24
  86.1 7.3 %collective-permute-start.8 = (f32[1,128,128]{2,1,0:T(8,128)S(1)}, f32[1,128,128]{2,1,0:T(8,128)S(1)}, u32[]{:S(2)}, u32[]{:S(2)}) collective-permute-start(f32[1,128,128]{2,1,0:T(8,128)S(1)} %get-tuple-element.12), channel_id=1, source_target_pairs={{1,0},{2,1},{3,2},{4,3},{5,4},{6,5},{7,6},{8,7},{9,8},{10,9},{11,1... | collective-permute-start | bytes 196616 | tf_op jit(solution)/shard_map/ppermute | solution.py:26
  93.4 1.8 %collective-permute-done.8 = f32[1,128,128]{2,1,0:T(8,128)S(1)} collective-permute-done((f32[1,128,128]{2,1,0:T(8,128)S(1)}, f32[1,128,128]{2,1,0:T(8,128)S(1)}, u32[]{:S(2)}, u32[]{:S(2)}) %collective-permute-start.8) | collective-permute-done | bytes 65568 | tf_op jit(solution)/shard_map/ppermute | solution.py:26
  95.2 0.1 select_maximum_fusion.6
  95.3 0.5 fusion.100
  95.8 1.9 %collective-permute-start.11 = (f32[1,128,128]{2,1,0:T(8,128)S(1)}, f32[1,128,128]{2,1,0:T(8,128)S(1)}, u32[]{:S(2)}, u32[]{:S(2)}) collective-permute-start(f32[1,128,128]{2,1,0:T(8,128)S(1)} %get-tuple-element.25), channel_id=1, source_target_pairs={{0,1},{1,2},{2,3},{3,4},{4,5},{5,6},{6,7},{7,8},{8,9},{9,10},{10,1... | collective-permute-start | bytes 196616 | tf_op jit(solution)/shard_map/ppermute | solution.py:24
  97.7 7.3 %collective-permute-start.10 = (f32[1,128,128]{2,1,0:T(8,128)S(1)}, f32[1,128,128]{2,1,0:T(8,128)S(1)}, u32[]{:S(2)}, u32[]{:S(2)}) collective-permute-start(f32[1,128,128]{2,1,0:T(8,128)S(1)} %get-tuple-element.26), channel_id=1, source_target_pairs={{1,0},{2,1},{3,2},{4,3},{5,4},{6,5},{7,6},{8,7},{9,8},{10,9},{11,1... | collective-permute-start | bytes 196616 | tf_op jit(solution)/shard_map/ppermute | solution.py:26
  105.0 0.0 collective-permute-done.11
  105.0 1.9 %collective-permute-done.10 = f32[1,128,128]{2,1,0:T(8,128)S(1)} collective-permute-done((f32[1,128,128]{2,1,0:T(8,128)S(1)}, f32[1,128,128]{2,1,0:T(8,128)S(1)}, u32[]{:S(2)}, u32[]{:S(2)}) %collective-permute-start.10) | collective-permute-done | bytes 65568 | tf_op jit(solution)/shard_map/ppermute | solution.py:26
  106.9 0.1 select_maximum_fusion.4
  107.0 0.6 fusion.23
  107.6 1.9 %collective-permute-start.13 = (f32[1,128,128]{2,1,0:T(8,128)S(1)}, f32[1,128,128]{2,1,0:T(8,128)S(1)}, u32[]{:S(2)}, u32[]{:S(2)}) collective-permute-start(f32[1,128,128]{2,1,0:T(8,128)S(1)} %get-tuple-element.23), channel_id=1, source_target_pairs={{0,1},{1,2},{2,3},{3,4},{4,5},{5,6},{6,7},{7,8},{8,9},{9,10},{10,1... | collective-permute-start | bytes 196616 | tf_op jit(solution)/shard_map/ppermute | solution.py:24
  109.5 7.3 %collective-permute-start.12 = (f32[1,128,128]{2,1,0:T(8,128)S(1)}, f32[1,128,128]{2,1,0:T(8,128)S(1)}, u32[]{:S(2)}, u32[]{:S(2)}) collective-permute-start(f32[1,128,128]{2,1,0:T(8,128)S(1)} %get-tuple-element.24), channel_id=1, source_target_pairs={{1,0},{2,1},{3,2},{4,3},{5,4},{6,5},{7,6},{8,7},{9,8},{10,9},{11,1... | collective-permute-start | bytes 196616 | tf_op jit(solution)/shard_map/ppermute | solution.py:26
  116.9 0.0 collective-permute-done.13
  116.9 1.9 %collective-permute-done.12 = f32[1,128,128]{2,1,0:T(8,128)S(1)} collective-permute-done((f32[1,128,128]{2,1,0:T(8,128)S(1)}, f32[1,128,128]{2,1,0:T(8,128)S(1)}, u32[]{:S(2)}, u32[]{:S(2)}) %collective-permute-start.12) | collective-permute-done | bytes 65568 | tf_op jit(solution)/shard_map/ppermute | solution.py:26
  118.7 0.1 select_maximum_fusion.2
  118.8 0.6 fusion.33
  119.4 1.9 %collective-permute-start.15 = (f32[1,128,128]{2,1,0:T(8,128)S(1)}, f32[1,128,128]{2,1,0:T(8,128)S(1)}, u32[]{:S(2)}, u32[]{:S(2)}) collective-permute-start(f32[1,128,128]{2,1,0:T(8,128)S(1)} %get-tuple-element.21), channel_id=1, source_target_pairs={{0,1},{1,2},{2,3},{3,4},{4,5},{5,6},{6,7},{7,8},{8,9},{9,10},{10,1... | collective-permute-start | bytes 196616 | tf_op jit(solution)/shard_map/ppermute | solution.py:24
  121.4 7.7 %collective-permute-start.14 = (f32[1,128,128]{2,1,0:T(8,128)S(1)}, f32[1,128,128]{2,1,0:T(8,128)S(1)}, u32[]{:S(2)}, u32[]{:S(2)}) collective-permute-start(f32[1,128,128]{2,1,0:T(8,128)S(1)} %get-tuple-element.22), channel_id=1, source_target_pairs={{1,0},{2,1},{3,2},{4,3},{5,4},{6,5},{7,6},{8,7},{9,8},{10,9},{11,1... | collective-permute-start | bytes 196616 | tf_op jit(solution)/shard_map/ppermute | solution.py:26
  129.1 0.4 collective-permute-done.15
  129.4 1.5 collective-permute-done.14
  130.9 0.1 select_maximum_fusion
  131.0 0.6 fusion.102
  131.6 0.3 copy.26
  131.9 16.0 %all_to_all.31 = f32[1,8,128,128]{3,1,0,2:T(8,128)S(1)} all-to-all(f32[1,8,128,128]{3,1,0,2:T(8,128)S(1)} %copy.26), channel_id=1, replica_groups=mesh['group'=16,'space'=32] {'group'}, dimensions={2} | all-to-all | bytes 1048576 | tf_op jit(solution)/shard_map/all_to_all | solution.py:127
  148.0 0.3 copy.29
  148.3 5.0 %collective-permute-start.17 = (f32[32,1,128]{2,1,0:T(1,128)S(1)}, f32[32,1,128]{2,1,0:T(1,128)S(1)}, u32[]{:S(2)}, u32[]{:S(2)}) collective-permute-start(f32[32,1,128]{2,1,0:T(1,128)S(1)} %get-tuple-element.19), channel_id=1, source_target_pairs={{32,0},{64,32},{96,64},{128,96},{160,128},{192,160},{224,192},{256... | collective-permute-start | bytes 49160 | tf_op jit(solution)/shard_map/ppermute | solution.py:26
  153.3 1.9 %collective-permute-start.16 = (f32[32,1,128]{2,1,0:T(1,128)S(1)}, f32[32,1,128]{2,1,0:T(1,128)S(1)}, u32[]{:S(2)}, u32[]{:S(2)}) collective-permute-start(f32[32,1,128]{2,1,0:T(1,128)S(1)} %get-tuple-element.20), channel_id=1, source_target_pairs={{0,32},{32,64},{64,96},{96,128},{128,160},{160,192},{192,224},{224... | collective-permute-start | bytes 49160 | tf_op jit(solution)/shard_map/ppermute | solution.py:24
  155.3 5.8 %collective-permute-done.16 = f32[32,1,128]{2,1,0:T(1,128)S(1)} collective-permute-done((f32[32,1,128]{2,1,0:T(1,128)S(1)}, f32[32,1,128]{2,1,0:T(1,128)S(1)}, u32[]{:S(2)}, u32[]{:S(2)}) %collective-permute-start.16) | collective-permute-done | bytes 16416 | tf_op jit(solution)/shard_map/ppermute | solution.py:24
  161.1 5.9 %collective-permute-start.18 = (f32[1,34,128]{2,1,0:T(8,128)S(1)}, f32[1,34,128]{2,1,0:T(8,128)S(1)}, u32[]{:S(2)}, u32[]{:S(2)}) collective-permute-start(f32[1,34,128]{2,1,0:T(8,128)S(1)} %get-tuple-element.15), channel_id=1, source_target_pairs={{1,0},{2,1},{3,2},{4,3},{5,4},{6,5},{7,6},{8,7},{9,8},{10,9},{11,1... | collective-permute-start | bytes 52232 | tf_op jit(solution)/shard_map/ppermute | solution.py:26
  167.0 1.9 %collective-permute-start.19 = (f32[1,34,128]{2,1,0:T(8,128)S(1)}, f32[1,34,128]{2,1,0:T(8,128)S(1)}, u32[]{:S(2)}, u32[]{:S(2)}) collective-permute-start(f32[1,34,128]{2,1,0:T(8,128)S(1)} %get-tuple-element.16), channel_id=1, source_target_pairs={{0,1},{1,2},{2,3},{3,4},{4,5},{5,6},{6,7},{7,8},{8,9},{9,10},{10,1... | collective-permute-start | bytes 52232 | tf_op jit(solution)/shard_map/ppermute | solution.py:24
  168.9 6.8 %collective-permute-done.19 = f32[1,34,128]{2,1,0:T(8,128)S(1)} collective-permute-done((f32[1,34,128]{2,1,0:T(8,128)S(1)}, f32[1,34,128]{2,1,0:T(8,128)S(1)}, u32[]{:S(2)}, u32[]{:S(2)}) %collective-permute-start.19) | collective-permute-done | bytes 17440 | tf_op jit(solution)/shard_map/ppermute | solution.py:24
  175.7 1.0 fusion.48
  (21 shorter events, 0.3 us)
Async XLA Ops:
  0.6 0.9 copy-start
  0.6 17.1 %copy-start.2 = (f32[32,32,128]{2,1,0:T(8,128)S(1)}, f32[32,32,128]{2,1,0:T(8,128)}, u32[]{:S(2)}) copy-start(f32[32,32,128]{2,1,0:T(8,128)} %param.4) | copy-start | bytes 1572868
  3.0 13.2 %collective-permute-start = (f32[2,32,1,128]{3,2,1,0:T(1,128)S(1)}, f32[2,32,1,128]{3,2,1,0:T(1,128)S(1)}, u32[]{:S(2)}, u32[]{:S(2)}) collective-permute-start(f32[2,32,1,128]{3,2,1,0:T(1,128)S(1)} %get-tuple-element.13), channel_id=1, source_target_pairs={{0,32},{32,64},{64,96},{96,128},{128,160},{160,192},{192,224},{224... | collective-permute-start | bytes 98312 | tf_op jit(solution)/shard_map/ppermute | solution.py:24
  7.3 10.4 %collective-permute-start.1 = (f32[2,32,1,128]{3,2,1,0:T(1,128)S(1)}, f32[2,32,1,128]{3,2,1,0:T(1,128)S(1)}, u32[]{:S(2)}, u32[]{:S(2)}) collective-permute-start(f32[2,32,1,128]{3,2,1,0:T(1,128)S(1)} %get-tuple-element.14), channel_id=1, source_target_pairs={{32,0},{64,32},{96,64},{128,96},{160,128},{192,160},{224,192},{256... | collective-permute-start | bytes 98312 | tf_op jit(solution)/shard_map/ppermute | solution.py:26
  17.7 9.2 %collective-permute-start.2 = (f32[2,1,34,128]{3,2,1,0:T(8,128)S(1)}, f32[2,1,34,128]{3,2,1,0:T(8,128)S(1)}, u32[]{:S(2)}, u32[]{:S(2)}) collective-permute-start(f32[2,1,34,128]{3,2,1,0:T(8,128)S(1)} %get-tuple-element.9), channel_id=1, source_target_pairs={{0,1},{1,2},{2,3},{3,4},{4,5},{5,6},{6,7},{7,8},{8,9},{9,10},{10,1... | collective-permute-start | bytes 104456 | tf_op jit(solution)/shard_map/ppermute | solution.py:24
  19.7 8.9 %collective-permute-start.3 = (f32[2,1,34,128]{3,2,1,0:T(8,128)S(1)}, f32[2,1,34,128]{3,2,1,0:T(8,128)S(1)}, u32[]{:S(2)}, u32[]{:S(2)}) collective-permute-start(f32[2,1,34,128]{3,2,1,0:T(8,128)S(1)} %get-tuple-element.10), channel_id=1, source_target_pairs={{1,0},{2,1},{3,2},{4,3},{5,4},{6,5},{7,6},{8,7},{9,8},{10,9},{11,1... | collective-permute-start | bytes 104456 | tf_op jit(solution)/shard_map/ppermute | solution.py:26
  28.9 1.0 copy-start.3
  30.7 29.6 %copy-start.1 = (f32[32,32,128]{2,1,0:T(8,128)}, f32[32,32,128]{2,1,0:T(8,128)S(1)}, u32[]{:S(2)}) copy-start(f32[32,32,128]{2,1,0:T(8,128)S(1)} %fusion.6) | copy-start | bytes 1572868
  30.8 8.3 %collective-permute-start.5 = (f32[32,1,128]{2,1,0:T(1,128)S(1)}, f32[32,1,128]{2,1,0:T(1,128)S(1)}, u32[]{:S(2)}, u32[]{:S(2)}) collective-permute-start(f32[32,1,128]{2,1,0:T(1,128)S(1)} %get-tuple-element.27), channel_id=1, source_target_pairs={{32,0},{64,32},{96,64},{128,96},{160,128},{192,160},{224,192},{256... | collective-permute-start | bytes 49160 | tf_op jit(solution)/shard_map/ppermute | solution.py:26
  37.1 7.7 %collective-permute-start.4 = (f32[32,1,128]{2,1,0:T(1,128)S(1)}, f32[32,1,128]{2,1,0:T(1,128)S(1)}, u32[]{:S(2)}, u32[]{:S(2)}) collective-permute-start(f32[32,1,128]{2,1,0:T(1,128)S(1)} %get-tuple-element.28), channel_id=1, source_target_pairs={{0,32},{32,64},{64,96},{96,128},{128,160},{160,192},{192,224},{224... | collective-permute-start | bytes 49160 | tf_op jit(solution)/shard_map/ppermute | solution.py:24
  44.8 8.4 %collective-permute-start.6 = (f32[1,34,128]{2,1,0:T(8,128)S(1)}, f32[1,34,128]{2,1,0:T(8,128)S(1)}, u32[]{:S(2)}, u32[]{:S(2)}) collective-permute-start(f32[1,34,128]{2,1,0:T(8,128)S(1)} %get-tuple-element.17), channel_id=1, source_target_pairs={{1,0},{2,1},{3,2},{4,3},{5,4},{6,5},{7,6},{8,7},{9,8},{10,9},{11,1... | collective-permute-start | bytes 52232 | tf_op jit(solution)/shard_map/ppermute | solution.py:26
  51.3 8.8 %collective-permute-start.7 = (f32[1,34,128]{2,1,0:T(8,128)S(1)}, f32[1,34,128]{2,1,0:T(8,128)S(1)}, u32[]{:S(2)}, u32[]{:S(2)}) collective-permute-start(f32[1,34,128]{2,1,0:T(8,128)S(1)} %get-tuple-element.18), channel_id=1, source_target_pairs={{0,1},{1,2},{2,3},{3,4},{4,5},{5,6},{6,7},{7,8},{8,9},{9,10},{10,1... | collective-permute-start | bytes 52232 | tf_op jit(solution)/shard_map/ppermute | solution.py:24
  84.2 9.2 %collective-permute-start.9 = (f32[1,128,128]{2,1,0:T(8,128)S(1)}, f32[1,128,128]{2,1,0:T(8,128)S(1)}, u32[]{:S(2)}, u32[]{:S(2)}) collective-permute-start(f32[1,128,128]{2,1,0:T(8,128)S(1)} %get-tuple-element.11), channel_id=1, source_target_pairs={{0,1},{1,2},{2,3},{3,4},{4,5},{5,6},{6,7},{7,8},{8,9},{9,10},{10,1... | collective-permute-start | bytes 196616 | tf_op jit(solution)/shard_map/ppermute | solution.py:24
  86.1 9.1 %collective-permute-start.8 = (f32[1,128,128]{2,1,0:T(8,128)S(1)}, f32[1,128,128]{2,1,0:T(8,128)S(1)}, u32[]{:S(2)}, u32[]{:S(2)}) collective-permute-start(f32[1,128,128]{2,1,0:T(8,128)S(1)} %get-tuple-element.12), channel_id=1, source_target_pairs={{1,0},{2,1},{3,2},{4,3},{5,4},{6,5},{7,6},{8,7},{9,8},{10,9},{11,1... | collective-permute-start | bytes 196616 | tf_op jit(solution)/shard_map/ppermute | solution.py:26
  95.8 9.2 %collective-permute-start.11 = (f32[1,128,128]{2,1,0:T(8,128)S(1)}, f32[1,128,128]{2,1,0:T(8,128)S(1)}, u32[]{:S(2)}, u32[]{:S(2)}) collective-permute-start(f32[1,128,128]{2,1,0:T(8,128)S(1)} %get-tuple-element.25), channel_id=1, source_target_pairs={{0,1},{1,2},{2,3},{3,4},{4,5},{5,6},{6,7},{7,8},{8,9},{9,10},{10,1... | collective-permute-start | bytes 196616 | tf_op jit(solution)/shard_map/ppermute | solution.py:24
  97.7 9.2 %collective-permute-start.10 = (f32[1,128,128]{2,1,0:T(8,128)S(1)}, f32[1,128,128]{2,1,0:T(8,128)S(1)}, u32[]{:S(2)}, u32[]{:S(2)}) collective-permute-start(f32[1,128,128]{2,1,0:T(8,128)S(1)} %get-tuple-element.26), channel_id=1, source_target_pairs={{1,0},{2,1},{3,2},{4,3},{5,4},{6,5},{7,6},{8,7},{9,8},{10,9},{11,1... | collective-permute-start | bytes 196616 | tf_op jit(solution)/shard_map/ppermute | solution.py:26
  107.6 9.2 %collective-permute-start.13 = (f32[1,128,128]{2,1,0:T(8,128)S(1)}, f32[1,128,128]{2,1,0:T(8,128)S(1)}, u32[]{:S(2)}, u32[]{:S(2)}) collective-permute-start(f32[1,128,128]{2,1,0:T(8,128)S(1)} %get-tuple-element.23), channel_id=1, source_target_pairs={{0,1},{1,2},{2,3},{3,4},{4,5},{5,6},{6,7},{7,8},{8,9},{9,10},{10,1... | collective-permute-start | bytes 196616 | tf_op jit(solution)/shard_map/ppermute | solution.py:24
  109.5 9.2 %collective-permute-start.12 = (f32[1,128,128]{2,1,0:T(8,128)S(1)}, f32[1,128,128]{2,1,0:T(8,128)S(1)}, u32[]{:S(2)}, u32[]{:S(2)}) collective-permute-start(f32[1,128,128]{2,1,0:T(8,128)S(1)} %get-tuple-element.24), channel_id=1, source_target_pairs={{1,0},{2,1},{3,2},{4,3},{5,4},{6,5},{7,6},{8,7},{9,8},{10,9},{11,1... | collective-permute-start | bytes 196616 | tf_op jit(solution)/shard_map/ppermute | solution.py:26
  119.4 10.0 %collective-permute-start.15 = (f32[1,128,128]{2,1,0:T(8,128)S(1)}, f32[1,128,128]{2,1,0:T(8,128)S(1)}, u32[]{:S(2)}, u32[]{:S(2)}) collective-permute-start(f32[1,128,128]{2,1,0:T(8,128)S(1)} %get-tuple-element.21), channel_id=1, source_target_pairs={{0,1},{1,2},{2,3},{3,4},{4,5},{5,6},{6,7},{7,8},{8,9},{9,10},{10,1... | collective-permute-start | bytes 196616 | tf_op jit(solution)/shard_map/ppermute | solution.py:24
  121.4 9.6 %collective-permute-start.14 = (f32[1,128,128]{2,1,0:T(8,128)S(1)}, f32[1,128,128]{2,1,0:T(8,128)S(1)}, u32[]{:S(2)}, u32[]{:S(2)}) collective-permute-start(f32[1,128,128]{2,1,0:T(8,128)S(1)} %get-tuple-element.22), channel_id=1, source_target_pairs={{1,0},{2,1},{3,2},{4,3},{5,4},{6,5},{7,6},{8,7},{9,8},{10,9},{11,1... | collective-permute-start | bytes 196616 | tf_op jit(solution)/shard_map/ppermute | solution.py:26
  148.3 6.9 %collective-permute-start.17 = (f32[32,1,128]{2,1,0:T(1,128)S(1)}, f32[32,1,128]{2,1,0:T(1,128)S(1)}, u32[]{:S(2)}, u32[]{:S(2)}) collective-permute-start(f32[32,1,128]{2,1,0:T(1,128)S(1)} %get-tuple-element.19), channel_id=1, source_target_pairs={{32,0},{64,32},{96,64},{128,96},{160,128},{192,160},{224,192},{256... | collective-permute-start | bytes 49160 | tf_op jit(solution)/shard_map/ppermute | solution.py:26
  153.3 7.7 %collective-permute-start.16 = (f32[32,1,128]{2,1,0:T(1,128)S(1)}, f32[32,1,128]{2,1,0:T(1,128)S(1)}, u32[]{:S(2)}, u32[]{:S(2)}) collective-permute-start(f32[32,1,128]{2,1,0:T(1,128)S(1)} %get-tuple-element.20), channel_id=1, source_target_pairs={{0,32},{32,64},{64,96},{96,128},{128,160},{160,192},{192,224},{224... | collective-permute-start | bytes 49160 | tf_op jit(solution)/shard_map/ppermute | solution.py:24
  161.1 7.9 %collective-permute-start.18 = (f32[1,34,128]{2,1,0:T(8,128)S(1)}, f32[1,34,128]{2,1,0:T(8,128)S(1)}, u32[]{:S(2)}, u32[]{:S(2)}) collective-permute-start(f32[1,34,128]{2,1,0:T(8,128)S(1)} %get-tuple-element.15), channel_id=1, source_target_pairs={{1,0},{2,1},{3,2},{4,3},{5,4},{6,5},{7,6},{8,7},{9,8},{10,9},{11,1... | collective-permute-start | bytes 52232 | tf_op jit(solution)/shard_map/ppermute | solution.py:26
  167.0 8.7 %collective-permute-start.19 = (f32[1,34,128]{2,1,0:T(8,128)S(1)}, f32[1,34,128]{2,1,0:T(8,128)S(1)}, u32[]{:S(2)}, u32[]{:S(2)}) collective-permute-start(f32[1,34,128]{2,1,0:T(8,128)S(1)} %get-tuple-element.16), channel_id=1, source_target_pairs={{0,1},{1,2},{2,3},{3,4},{4,5},{5,6},{6,7},{7,8},{8,9},{9,10},{10,1... | collective-permute-start | bytes 52232 | tf_op jit(solution)/shard_map/ppermute | solution.py:24
where the time goes:
time: 178 us; the launch traced here: 177 us
  starting transfers between devices  90.9 us (51%)
  blocking collectives  39.5 us (22%)
  waiting for transfers between devices  35.9 us (20%)
  other arithmetic  5.85 us (3%)
  local copies, waits for them, and re-layouts  3.06 us (2%)
    ppermute x10, starting transfers between devices, padded_2(): lax.ppermute(head, axis, [((i + 1) % count, i) for i in range(ends)])  69.3 us
    ppermute x10, waiting for transfers between devices, padded_2(): lax.ppermute(tail, axis, [(i, (i + 1) % count) for i in range(ends)])  25.6 us
    all_to_all x1, blocking collectives, per_device(): lax.all_to_all(packed, 'group', split_axis=1, concat_axis=3, tiled=True)  23.4 us
    ppermute x10, starting transfers between devices, padded_2(): lax.ppermute(tail, axis, [(i, (i + 1) % count) for i in range(ends)])  21.6 us
    all_to_all x1, blocking collectives, per_device(): lax.all_to_all(iterate[None], 'group', split_axis=2, concat_axis=0, tiled...  16 us
    ppermute x10, waiting for transfers between devices, padded_2(): lax.ppermute(head, axis, [((i + 1) % count, i) for i in range(ends)])  10.3 us
  transfers between devices with their start and end apart: 20, of which 11 were waited for; matrix products, arithmetic and copies ran while one was open for 0% of the time, Pallas kernels for 0%

commit v1 on v0

v1 whole, which is shorter than its diff:
```python
import jax
import jax.numpy as jnp
from jax import lax
from jax.experimental import pallas as pl
from jax.experimental.pallas import tpu as pltpu
from jax.sharding import PartitionSpec as P

MESH = pl.DeviceIdType.MESH
N = 32
DEPTH = 128
XO, YO = 17, 20
NXF, NYF = 66, 72
DIRS = [(dx, dy) for dx in (-1, 0, 1) for dy in (-1, 0, 1) if (dx, dy) != (0, 0)]
SIDES = [(-1, 0), (1, 0), (0, -1), (0, 1)]


def span(step, width, origin):
    if step == 1:
        return origin + N - width, origin - width
    if step == -1:
        return origin, origin + N
    return origin, origin


def kernel(p_hbm, src_hbm, lab_hbm, tab_hbm, res_hbm, cor_hbm,
           pb, sb, tb, lb, lt, rb, s_ref, w_ref, k_ref, ua, pa, ub, qb, uc, ob,
           send, recv, local):
    groups = lax.axis_size("group")
    spaces = lax.axis_size("space")
    gi = lax.axis_index("group")
    si = lax.axis_index("space")

    def there(d):
        dx, dy = d
        ok = None
        if dx == 1:
            ok = si < spaces - 1
        elif dx == -1:
            ok = si > 0
        if dy:
            okg = gi < groups - 1 if dy == 1 else gi > 0
            ok = okg if ok is None else jnp.logical_and(ok, okg)
        return ok

    def back(d):
        return (-d[0], -d[1])

    def device(d):
        return (gi + d[1], si + d[0])

    load_p = pltpu.make_async_copy(p_hbm, pb.at[pl.ds(1, N), pl.ds(4, N), :], local.at[0])
    load_s = pltpu.make_async_copy(src_hbm, sb, local.at[1])
    load_l = pltpu.make_async_copy(lab_hbm, lb.at[1, pl.ds(N, N), :], local.at[2])
    load_t = pltpu.make_async_copy(tab_hbm, tb, local.at[3])
    load_l.start()
    load_t.start()
    load_p.start()
    load_s.start()

    barrier = pltpu.get_barrier_semaphore()
    count = jnp.int32(0)
    for d in DIRS:
        ok = there(d)
        count = count + ok.astype(jnp.int32)

        @pl.when(ok)
        def _():
            pl.semaphore_signal(barrier, 1, device_id=device(d), device_id_type=MESH)

    for d in DIRS:
        @pl.when(jnp.logical_not(there(d)))
        def _():
            dx, dy = d
            lb[1 + dy, pl.ds(N * (1 + dx), N), :] = jnp.full((N, N), -1, jnp.int32)

    for d in SIDES:
        @pl.when(jnp.logical_not(there(d)))
        def _():
            dx, dy = d
            if dx:
                pb[0 if dx < 0 else N + 1] = jnp.zeros((40, DEPTH), jnp.float32)
                r0 = XO - 14 if dx < 0 else XO + N

                @pl.loop(0, 14)
                def _(i):
                    rb[r0 + i] = jnp.zeros((NYF, DEPTH), jnp.float32)
            else:
                col = 3 if dy < 0 else 4 + N
                pb[pl.ds(1, N), pl.ds(col, 1), :] = jnp.zeros((N, 1, DEPTH), jnp.float32)
                c0 = YO - 14 if dy < 0 else YO + N

                @pl.loop(XO - 14, XO + N + 14)
                def _(i):
                    rb[i, pl.ds(c0, 14), :] = jnp.zeros((14, DEPTH), jnp.float32)

    pl.semaphore_wait(barrier, count)

    def message(kind, d):
        dx, dy = d
        if kind == 0:
            at = DIRS.index(d)
            src = lab_hbm
            dst = lb.at[1 - dy, pl.ds(N * (1 - dx), N), :]
        elif kind == 1:
            at = 8 + SIDES.index(d)
            if dx:
                src = p_hbm.at[pl.ds(N - 1 if dx > 0 else 0, 1)]
                dst = pb.at[pl.ds(0 if dx > 0 else N + 1, 1), pl.ds(4, N), :]
            else:
                src = p_hbm.at[:, pl.ds(N - 1 if dy > 0 else 0, 1), :]
                dst = pb.at[pl.ds(1, N), pl.ds(3 if dy > 0 else 4 + N, 1), :]
        else:
            at = 12 + DIRS.index(d)
            wide = 14 if dx == 0 or dy == 0 else 13
            sx, tx = span(dx, wide, XO)
            sy, ty = span(dy, wide, YO)
            nx = wide if dx else N
            ny = wide if dy else N
            src = rb.at[pl.ds(sx, nx), pl.ds(sy, ny), :]
            dst = rb.at[pl.ds(tx, nx), pl.ds(ty, ny), :]
        return pltpu.make_async_remote_copy(
            src_ref=src, dst_ref=dst, send_sem=send.at[at], recv_sem=recv.at[at],
            device_id=device(d), device_id_type=MESH)

    def start(kind, dirs):
        for d in dirs:
            @pl.when(there(d))
            def _():
                message(kind, d).start()

    def arrive(kind, dirs):
        for d in dirs:
            @pl.when(there(back(d)))
            def _():
                message(kind, d).wait_recv()

    def sent(kind, dirs):
        for d in dirs:
            @pl.when(there(d))
            def _():
                message(kind, d).wait_send()

    start(1, SIDES)
    start(0, DIRS)

    load_t.wait()
    half = 0.5 * tb[...]
    lane = lax.broadcasted_iota(jnp.int32, (16, DEPTH), 1)
    up = jnp.where(lane < DEPTH - 1, pltpu.roll(half, DEPTH - 1, 1), 0.0)
    down = jnp.where(lane > 0, pltpu.roll(half, 1, 1), 0.0)
    wup = jnp.where(lane < DEPTH - 1, half + up, 0.0)
    vert = 6.0 * half + (up + down)
    wide = jnp.concatenate([half, wup, vert], axis=1)
    hi = wide.astype(jnp.bfloat16)
    rest = wide - hi.astype(jnp.float32)
    mid = rest.astype(jnp.bfloat16)
    low = (rest - mid.astype(jnp.float32)).astype(jnp.bfloat16)
    table = jnp.concatenate(
        [hi, mid, low, jnp.zeros((DEPTH - 48, 3 * DEPTH), jnp.bfloat16)], axis=0)

    load_l.wait()
    arrive(0, DIRS)
    t0 = lb[0].T
    t1 = lb[1].T
    t2 = lb[2].T
    pad = jnp.full((N, DEPTH - 96), -1, jnp.int32)
    lt[pl.ds(0, 20), :] = jnp.concatenate([t0, pad], axis=1)[12:]
    lt[pl.ds(20, N), :] = jnp.concatenate([t1, pad], axis=1)
    lt[pl.ds(52, 20), :] = jnp.concatenate([t2, pad], axis=1)[:20]

    lanes = lax.broadcasted_iota(jnp.int32, (NYF, DEPTH), 1)
    slot = jnp.where(lanes < 48, lanes & 15, -9)

    @pl.loop(0, NXF)
    def _(x):
        turned = pltpu.roll(lt[...], DEPTH - (x + N - XO), 1)
        tag = jnp.broadcast_to(turned[:, 0:1], (NYF, DEPTH))
        onehot = jnp.where(tag == slot, 1.0, 0.0).astype(jnp.bfloat16)
        out = jnp.dot(onehot, table, preferred_element_type=jnp.float32)
        s_ref[x] = out[:, :DEPTH]
        w_ref[x] = out[:, DEPTH:2 * DEPTH]
        k_ref[x] = out[:, 2 * DEPTH:]

    def vertical(weight, value):
        return weight * pltpu.roll(value, DEPTH - 1, 1) + pltpu.roll(weight * value, 1, 1)

    load_p.wait()
    load_s.wait()
    arrive(1, SIDES)

    @pl.loop(0, N)
    def _(x):
        fx = x + XO
        own = pl.ds(YO, N)
        s = s_ref[fx, own, :]
        sn = [s_ref[fx - 1, own, :], s_ref[fx + 1, own, :],
              s_ref[fx, pl.ds(YO - 1, N), :], s_ref[fx, pl.ds(YO + 1, N), :]]
        p = pb[x + 1, pl.ds(4, N), :]
        pn = [pb[x, pl.ds(4, N), :], pb[x + 2, pl.ds(4, N), :],
              pb[x + 1, pl.ds(3, N), :], pb[x + 1, pl.ds(5, N), :]]
        flow = (s + sn[0]) * (p - pn[0])
        for i in range(1, 4):
            flow = flow + (s + sn[i]) * (p - pn[i])
        both = k_ref[fx, own, :] - 4.0 * s
        flow = flow + (both * p - vertical(w_ref[fx, own, :], p))
        rb[fx, own, :] = sb[x] - flow

    start(2, DIRS)
    out_r = pltpu.make_async_copy(rb.at[pl.ds(XO, N), pl.ds(YO, N), :], res_hbm, local.at[4])
    out_r.start()

    @pl.loop(4, NXF - 4)
    def _(x):
        at = pl.ds(4, 64)
        s = s_ref[x, at, :]
        diag = (k_ref[x, at, :] + (s_ref[x - 4, at, :] + s_ref[x + 4, at, :])
                + (s_ref[x, pl.ds(0, 64), :] + s_ref[x, pl.ds(8, 64), :]))
        k_ref[x, at, :] = jnp.where(s > 0.0, 0.8 / diag, 0.0)

    arrive(2, DIRS)

    @pl.loop(4, NXF - 4)
    def _(x):
        at = pl.ds(4, 64)
        mean = (0.5 * rb[x, at, :]
                + 0.125 * (rb[x - 1, at, :] + rb[x + 1, at, :]
                           + rb[x, pl.ds(3, 64), :] + rb[x, pl.ds(5, 64), :]))
        u = k_ref[x, at, :] * mean
        sb2 = s_ref[x, at, :]
        ua[x, at, :] = u
        pa[x, at, :] = sb2 * u

    def sweep(first, u_in, p_in, u_out, p_out, base):
        y0, ny = first, NYF - 2 * first

        @pl.loop(first, NXF - first)
        def _(x):
            at = pl.ds(y0, ny)
            lo = pl.ds(y0 - 4, ny)
            hi_ = pl.ds(y0 + 4, ny)
            s = s_ref[x, at, :]
            u = u_in[x, at, :]
            un = (u_in[x - 4, at, :] + u_in[x + 4, at, :]
                  + u_in[x, lo, :] + u_in[x, hi_, :])
            pn = (p_in[x - 4, at, :] + p_in[x + 4, at, :]
                  + p_in[x, lo, :] + p_in[x, hi_, :])
            total = s * un + pn + vertical(w_ref[x, at, :], u)
            new = base[x, at, :] + 0.2 * u + k_ref[x, at, :] * total
            u_out[x, at, :] = new
            if p_out is not None:
                p_out[x, at, :] = s * new

    sweep(8, ua, pa, ub, qb, ua)
    sweep(12, ub, qb, uc, pa, ua)
    sweep(16, uc, pa, ub, None, ua)

    @pl.loop(0, N)
    def _(x):
        fx = x + XO
        at = pl.ds(YO, N)
        ob[x] = (0.5 * ub[fx, at, :]
                 + 0.125 * (ub[fx - 1, at, :] + ub[fx + 1, at, :]
                            + ub[fx, pl.ds(YO - 1, N), :] + ub[fx, pl.ds(YO + 1, N), :]))

    out_c = pltpu.make_async_copy(ob, cor_hbm, local.at[5])
    out_c.start()
    sent(0, DIRS)
    sent(1, SIDES)
    sent(2, DIRS)
    out_r.wait()
    out_c.wait()


def per_device(pressure, source, labels, region_table):
    any_ = pl.BlockSpec(memory_space=pl.ANY)
    own = jax.ShapeDtypeStruct((N, N, DEPTH), jnp.float32)
    field = pltpu.VMEM((NXF, NYF, DEPTH), jnp.float32)
    return pl.pallas_call(
        kernel,
        out_shape=(own, own),
        in_specs=[any_] * 4,
        out_specs=(any_, any_),
        scratch_shapes=[
            pltpu.VMEM((N + 2, 40, DEPTH), jnp.float32),
            pltpu.VMEM((N, N, DEPTH), jnp.float32),
            pltpu.VMEM((16, DEPTH), jnp.float32),
            pltpu.VMEM((3, 3 * N, N), jnp.int32),
            pltpu.VMEM((NYF, DEPTH), jnp.int32),
            field, field, field, field, field, field, field, field, field,
            pltpu.VMEM((N, N, DEPTH), jnp.float32),
            pltpu.SemaphoreType.DMA((20,)),
            pltpu.SemaphoreType.DMA((20,)),
            pltpu.SemaphoreType.DMA((6,)),
        ],
        compiler_params=pltpu.CompilerParams(collective_id=0, has_side_effects=True),
        name="correction",
    )(pressure, source, labels, region_table)


def solution(mesh):
    placed = (P("space", "group", None), P("space", "group", None), P("space", "group"), P())
    return jax.shard_map(
        per_device,
        mesh=mesh,
        in_specs=placed,
        out_specs=(P("space", "group", None), P("space", "group", None)),
        check_vma=False,
    )
```

time: 178 us -> 66.2 us (0.37)
  starting transfers between devices: 90.9 us -> 0 us
  Pallas kernels: 0 us -> 61.6 us
  blocking collectives: 39.5 us -> 0 us
  waiting for transfers between devices: 35.9 us -> 0 us
  other arithmetic: 5.85 us -> 0 us
    ppermute x20 -> x0, starting transfers between devices: 90.9 us -> none  [the longest x10 69.3 us: padded_2(): lax.ppermute(head, axis, [((i + 1) % count, i) for i in range(ends)])]
    pallas_call x0 -> x1, Pallas kernels: none -> 61.6 us  [per_device(): pl.pallas_call(kernel, out_shape=(own, own), in_specs=[any_] * 4, out_spe...]
    all_to_all x2 -> x0, blocking collectives: 39.5 us -> none  [the longest x1 23.4 us: per_device(): lax.all_to_all(packed, 'group', split_axis=1, concat_axis=3, tiled=True)]
    ppermute x20 -> x0, waiting for transfers between devices: 35.9 us -> none  [the longest x10 25.6 us: padded_2(): lax.ppermute(tail, axis, [(i, (i + 1) % count) for i in range(ends)])]
    add x4 -> x0, other arithmetic: 2.44 us -> none  [the longest x2 1.24 us: blend(): return centre_weight * centre + side_weight * sides]
    unnamed x8 -> x4, local copies, waits for them, and re-layouts: 0.92 us -> 2.72 us
  transfers between devices with their start and end apart: 20 -> 0, of which waited for: 11 -> 0; matrix products, arithmetic and copies ran while one was open for 0% -> 0% of each run, Pallas kernels for 0% -> 0%
where the time goes in v1:
time: 66.2 us; the launch traced here: 65 us
  Pallas kernels  61.6 us (93%)
  local copies, waits for them, and re-layouts  2.72 us (4%)
    pallas_call x1, Pallas kernels, per_device(): pl.pallas_call(kernel, out_shape=(own, own), in_specs=[any_] * 4, out_spe...  61.6 us
    unnamed x4, local copies, waits for them, and re-layouts  2.72 us

profile of v1, /device:TPU:6, one launch (start us, length us, event | category | flops | bytes accessed | tf_op | source)
XLA Modules:
  0.0 65.0 jit_solution(13756111166496183318)
XLA Ops:
  0.6 61.6 %correction.1 = (f32[32,32,128]{2,1,0:T(8,128)}, f32[32,32,128]{2,1,0:T(8,128)}) custom-call(f32[32,32,128]{2,1,0:T(8,128)} %p_hbm.1, f32[32,32,128]{2,1,0:T(8,128)} %src_hbm.1, s32[32,32]{1,0:T(8,128)} %lab_hbm.1, f32[16,128]{1,0:T(8,128)} %tab_hbm.1), custom_call_target="tpu_custom_call" | custom-call | tf_op jit(solution)/shard_map/correction/pallas_call | solution.py:278
  62.2 0.0 copy-start
  62.3 1.9 %copy.8 = f32[32,32,128]{2,1,0:T(8,128)} copy(f32[32,32,128]{2,1,0:T(8,128)} %get-tuple-element.4) | data formatting | bytes 1048576
  64.2 0.0 copy-done
  64.2 0.8 %copy.9 = f32[32,32,128]{2,1,0:T(8,128)} copy(f32[32,32,128]{2,1,0:T(8,128)S(1)} %copy-done) | data formatting | bytes 1048576
Async XLA Ops:
  62.2 1.9 %copy-start = (f32[32,32,128]{2,1,0:T(8,128)S(1)}, f32[32,32,128]{2,1,0:T(8,128)}, u32[]{:S(2)}) copy-start(f32[32,32,128]{2,1,0:T(8,128)} %get-tuple-element.5) | copy-start | bytes 1572868

commit v2 on v1

--- a/solution.py
+++ b/solution.py
@@ -22,9 +22,8 @@
     return origin, origin
 
 
-def kernel(p_hbm, src_hbm, lab_hbm, tab_hbm, res_hbm, cor_hbm,
-           pb, sb, tb, lb, lt, rb, s_ref, w_ref, k_ref, ua, pa, ub, qb, uc, ob,
-           send, recv, local):
+def exchange(p_hbm, src_hbm, lab_hbm, tab_hbm, s_ref, w_ref, k_ref, rb,
+             pb, sb, tb, lb, lt, send, recv, local):
     groups = lax.axis_size("group")
     spaces = lax.axis_size("space")
     gi = lax.axis_index("group")
@@ -158,31 +157,46 @@
     table = jnp.concatenate(
         [hi, mid, low, jnp.zeros((DEPTH - 48, 3 * DEPTH), jnp.bfloat16)], axis=0)
 
+    def tags(block):
+        pad = jnp.full((N, DEPTH - 3 * N), -1, jnp.int32)
+        return jnp.concatenate([block.T, pad], axis=1)
+
+    def coefficients(xs, y0, ny):
+        lanes = lax.broadcasted_iota(jnp.int32, (ny, DEPTH), 1)
+        slot = jnp.where(lanes < 48, lanes & 15, -9)
+        at = pl.ds(y0, ny)
+        tag = lt[at, :]
+        hits = []
+        for x in xs:
+            c = x + N - XO
+            hit = jnp.broadcast_to(tag[:, c:c + 1], (ny, DEPTH)) == slot
+            hits.append(jnp.where(hit, 1.0, 0.0))
+        onehot = jnp.concatenate(hits, axis=0).astype(jnp.bfloat16)
+        out = jnp.dot(onehot, table, preferred_element_type=jnp.float32)
+        for n, x in enumerate(xs):
+            part = out[n * ny:(n + 1) * ny]
+            s_ref[x, at, :] = part[:, :DEPTH]
+            w_ref[x, at, :] = part[:, DEPTH:2 * DEPTH]
+            k_ref[x, at, :] = part[:, 2 * DEPTH:]
+
+    own_x = list(range(XO, XO + N))
     load_l.wait()
+    none = jnp.full((N, N), -1, jnp.int32)
+    lt[pl.ds(20, N), :] = tags(jnp.concatenate([none, lb[1, pl.ds(N, N), :], none], axis=0))
+    coefficients(own_x, 16, 40)
+
     arrive(0, DIRS)
-    t0 = lb[0].T
-    t1 = lb[1].T
-    t2 = lb[2].T
-    pad = jnp.full((N, DEPTH - 96), -1, jnp.int32)
-    lt[pl.ds(0, 20), :] = jnp.concatenate([t0, pad], axis=1)[12:]
-    lt[pl.ds(20, N), :] = jnp.concatenate([t1, pad], axis=1)
-    lt[pl.ds(52, 20), :] = jnp.concatenate([t2, pad], axis=1)[:20]
-
-    lanes = lax.broadcasted_iota(jnp.int32, (NYF, DEPTH), 1)
-    slot = jnp.where(lanes < 48, lanes & 15, -9)
-
-    @pl.loop(0, NXF)
-    def _(x):
-        turned = pltpu.roll(lt[...], DEPTH - (x + N - XO), 1)
-        tag = jnp.broadcast_to(turned[:, 0:1], (NYF, DEPTH))
-        onehot = jnp.where(tag == slot, 1.0, 0.0).astype(jnp.bfloat16)
-        out = jnp.dot(onehot, table, preferred_element_type=jnp.float32)
-        s_ref[x] = out[:, :DEPTH]
-        w_ref[x] = out[:, DEPTH:2 * DEPTH]
-        k_ref[x] = out[:, 2 * DEPTH:]
+    lt[pl.ds(0, 20), :] = tags(lb[0])[12:]
+    lt[pl.ds(20, N), :] = tags(lb[1])
+    lt[pl.ds(52, 20), :] = tags(lb[2])[:20]
 
     def vertical(weight, value):
         return weight * pltpu.roll(value, DEPTH - 1, 1) + pltpu.roll(weight * value, 1, 1)
+
+    for part in (range(0, XO), range(XO + N, NXF)):
+        coefficients(list(part), 0, NYF)
+    coefficients(own_x, 0, 24)
+    coefficients(own_x, 48, 24)
 
     load_p.wait()
     load_s.wait()
@@ -206,9 +220,6 @@
         rb[fx, own, :] = sb[x] - flow
 
     start(2, DIRS)
-    out_r = pltpu.make_async_copy(rb.at[pl.ds(XO, N), pl.ds(YO, N), :], res_hbm, local.at[4])
-    out_r.start()
-
     @pl.loop(4, NXF - 4)
     def _(x):
         at = pl.ds(4, 64)
@@ -219,25 +230,36 @@
 
     arrive(2, DIRS)
 
-    @pl.loop(4, NXF - 4)
-    def _(x):
+    sent(0, DIRS)
+    sent(1, SIDES)
+    sent(2, DIRS)
+
+
+def relax(s_ref, w_ref, k_ref, rb, res_hbm, cor_hbm, ua, pa, ub, qb, uc, ob, local):
+    out_r = pltpu.make_async_copy(rb.at[pl.ds(XO, N), pl.ds(YO, N), :], res_hbm, local.at[0])
+    out_r.start()
+
+    def vertical(weight, value):
+        return weight * pltpu.roll(value, DEPTH - 1, 1) + pltpu.roll(weight * value, 1, 1)
+
+    @pl.loop(0, (NXF - 8) // 2)
+    def _(i):
         at = pl.ds(4, 64)
-        mean = (0.5 * rb[x, at, :]
-                + 0.125 * (rb[x - 1, at, :] + rb[x + 1, at, :]
-                           + rb[x, pl.ds(3, 64), :] + rb[x, pl.ds(5, 64), :]))
-        u = k_ref[x, at, :] * mean
-        sb2 = s_ref[x, at, :]
-        ua[x, at, :] = u
-        pa[x, at, :] = sb2 * u
+        for x in (4 + 2 * i, 5 + 2 * i):
+            mean = (0.5 * rb[x, at, :]
+                    + 0.125 * (rb[x - 1, at, :] + rb[x + 1, at, :]
+                               + rb[x, pl.ds(3, 64), :] + rb[x, pl.ds(5, 64), :]))
+            u = k_ref[x, at, :] * mean
+            ua[x, at, :] = u
+            pa[x, at, :] = s_ref[x, at, :] * u
 
     def sweep(first, u_in, p_in, u_out, p_out, base):
         y0, ny = first, NYF - 2 * first
-
-        @pl.loop(first, NXF - first)
-        def _(x):
-            at = pl.ds(y0, ny)
-            lo = pl.ds(y0 - 4, ny)
-            hi_ = pl.ds(y0 + 4, ny)
+        at = pl.ds(y0, ny)
+        lo = pl.ds(y0 - 4, ny)
+        hi_ = pl.ds(y0 + 4, ny)
+
+        def row(x):
             s = s_ref[x, at, :]
             u = u_in[x, at, :]
             un = (u_in[x - 4, at, :] + u_in[x + 4, at, :]
@@ -246,9 +268,16 @@
                   + p_in[x, lo, :] + p_in[x, hi_, :])
             total = s * un + pn + vertical(w_ref[x, at, :], u)
             new = base[x, at, :] + 0.2 * u + k_ref[x, at, :] * total
-            u_out[x, at, :] = new
-            if p_out is not None:
-                p_out[x, at, :] = s * new
+            return s, new
+
+        @pl.loop(0, (NXF - 2 * first) // 2)
+        def _(i):
+            xs = (first + 2 * i, first + 2 * i + 1)
+            out = [row(x) for x in xs]
+            for x, (s, new) in zip(xs, out):
+                u_out[x, at, :] = new
+                if p_out is not None:
+                    p_out[x, at, :] = s * new
 
     sweep(8, ua, pa, ub, qb, ua)
     sweep(12, ub, qb, uc, pa, ua)
@@ -262,39 +291,49 @@
                  + 0.125 * (ub[fx - 1, at, :] + ub[fx + 1, at, :]
                             + ub[fx, pl.ds(YO - 1, N), :] + ub[fx, pl.ds(YO + 1, N), :]))
 
-    out_c = pltpu.make_async_copy(ob, cor_hbm, local.at[5])
+    out_c = pltpu.make_async_copy(ob, cor_hbm, local.at[1])
     out_c.start()
-    sent(0, DIRS)
-    sent(1, SIDES)
-    sent(2, DIRS)
     out_r.wait()
     out_c.wait()
 
 
 def per_device(pressure, source, labels, region_table):
-    any_ = pl.BlockSpec(memory_space=pl.ANY)
+    hbm = pl.BlockSpec(memory_space=pltpu.HBM)
+    vmem = pl.BlockSpec(memory_space=pltpu.VMEM)
     own = jax.ShapeDtypeStruct((N, N, DEPTH), jnp.float32)
     field = pltpu.VMEM((NXF, NYF, DEPTH), jnp.float32)
-    return pl.pallas_call(
-        kernel,
-        out_shape=(own, own),
-        in_specs=[any_] * 4,
-        out_specs=(any_, any_),
+    fields = pl.pallas_call(
+        exchange,
+        out_shape=(field,) * 4,
+        in_specs=[hbm] * 4,
+        out_specs=(vmem,) * 4,
         scratch_shapes=[
             pltpu.VMEM((N + 2, 40, DEPTH), jnp.float32),
             pltpu.VMEM((N, N, DEPTH), jnp.float32),
             pltpu.VMEM((16, DEPTH), jnp.float32),
             pltpu.VMEM((3, 3 * N, N), jnp.int32),
             pltpu.VMEM((NYF, DEPTH), jnp.int32),
-            field, field, field, field, field, field, field, field, field,
-            pltpu.VMEM((N, N, DEPTH), jnp.float32),
             pltpu.SemaphoreType.DMA((20,)),
             pltpu.SemaphoreType.DMA((20,)),
-            pltpu.SemaphoreType.DMA((6,)),
+            pltpu.SemaphoreType.DMA((4,)),
         ],
-        compiler_params=pltpu.CompilerParams(collective_id=0, has_side_effects=True),
-        name="correction",
-    )(pressure, source, labels, region_table)
+        compiler_params=pltpu.CompilerParams(
+            collective_id=0, has_side_effects=True, vmem_limit_bytes=24 << 20),
+        name="exchange",
+    )(*[pltpu.with_memory_space_constraint(a, pltpu.HBM)
+        for a in (pressure, source, labels, region_table)])
+    return pl.pallas_call(
+        relax,
+        out_shape=(own, own),
+        in_specs=[vmem] * 4,
+        out_specs=(hbm, hbm),
+        scratch_shapes=[field] * 5 + [
+            pltpu.VMEM((N, N, DEPTH), jnp.float32),
+            pltpu.SemaphoreType.DMA((2,)),
+        ],
+        compiler_params=pltpu.CompilerParams(vmem_limit_bytes=24 << 20),
+        name="relax",
+    )(*fields)
 
 
 def solution(mesh):

time: 66.2 us -> 41.6 us (0.63)
  the two profiles are of different devices: /device:TPU:6 before, /device:TPU:31 now
where the time goes in v2:
time: 41.6 us; the launch traced here: 41.4 us
  Pallas kernels  40.8 us (98%)
  between operations  0.64 us (2%)
    pallas_call x1, Pallas kernels, per_device(): pl.pallas_call(exchange, out_shape=(field,) * 4, in_specs=[hbm] * 4, out_...  32.2 us
    pallas_call x1, Pallas kernels, per_device(): pl.pallas_call(relax, out_shape=(own, own), in_specs=[vmem] * 4, out_spec...  8.58 us

profile of v2, /device:TPU:31, one launch (start us, length us, event | category | flops | bytes accessed | tf_op | source)
XLA Modules:
  0.0 41.4 jit_solution(2986392865839967606)
XLA Ops:
  0.6 32.2 %exchange.1 = (f32[66,72,128]{2,1,0:T(8,128)S(1)}, f32[66,72,128]{2,1,0:T(8,128)S(1)}, f32[66,72,128]{2,1,0:T(8,128)S(1)}, f32[66,72,128]{2,1,0:T(8,128)S(1)}) custom-call(f32[32,32,128]{2,1,0:T(8,128)} %p_hbm.1, f32[32,32,128]{2,1,0:T(8,128)} %src_hbm.1, s32[32,32]{1,0:T(8,128)} %lab_hbm.1, f32[16,128]{1,0:T(8,128)} %tab_hbm.1), custom_call_target="tpu_custom_call" | custom-call | tf_op jit(solution)/shard_map/exchange/pallas_call | solution.py:305
  32.8 8.6 %relax.1 = (f32[32,32,128]{2,1,0:T(8,128)}, f32[32,32,128]{2,1,0:T(8,128)}) custom-call(f32[66,72,128]{2,1,0:T(8,128)S(1)} %get-tuple-element.6.s_ref, f32[66,72,128]{2,1,0:T(8,128)S(1)} %get-tuple-element.7.w_ref, f32[66,72,128]{2,1,0:T(8,128)S(1)} %get-tuple-element.8.k_ref, f32[66,72,128]{2,1,0:T(8,128)S(1)} %get-tuple-element.9.rb), custom_call_target="tpu_custom_call" | custom-call | tf_op jit(solution)/shard_map/relax/pallas_call | solution.py:325

commit v3 on v2

--- a/solution.py
+++ b/solution.py
@@ -10,6 +10,7 @@
 DEPTH = 128
 XO, YO = 17, 20
 NXF, NYF = 66, 72
+R1, R2, R3 = 10, 7, 7
 DIRS = [(dx, dy) for dx in (-1, 0, 1) for dy in (-1, 0, 1) if (dx, dy) != (0, 0)]
 SIDES = [(-1, 0), (1, 0), (0, -1), (0, 1)]
 
@@ -23,7 +24,7 @@
 
 
 def exchange(p_hbm, src_hbm, lab_hbm, tab_hbm, s_ref, w_ref, k_ref, rb,
-             pb, sb, tb, lb, lt, send, recv, local):
+             pb, sb, tb, lb, lt, hx, hy, send, recv, local):
     groups = lax.axis_size("group")
     spaces = lax.axis_size("space")
     gi = lax.axis_index("group")
@@ -77,15 +78,12 @@
         def _():
             dx, dy = d
             if dx:
-                pb[0 if dx < 0 else N + 1] = jnp.zeros((40, DEPTH), jnp.float32)
                 r0 = XO - 14 if dx < 0 else XO + N
 
                 @pl.loop(0, 14)
                 def _(i):
                     rb[r0 + i] = jnp.zeros((NYF, DEPTH), jnp.float32)
             else:
-                col = 3 if dy < 0 else 4 + N
-                pb[pl.ds(1, N), pl.ds(col, 1), :] = jnp.zeros((N, 1, DEPTH), jnp.float32)
                 c0 = YO - 14 if dy < 0 else YO + N
 
                 @pl.loop(XO - 14, XO + N + 14)
@@ -103,11 +101,11 @@
         elif kind == 1:
             at = 8 + SIDES.index(d)
             if dx:
-                src = p_hbm.at[pl.ds(N - 1 if dx > 0 else 0, 1)]
-                dst = pb.at[pl.ds(0 if dx > 0 else N + 1, 1), pl.ds(4, N), :]
+                src = p_hbm.at[N - 1 if dx > 0 else 0]
+                dst = hx.at[0 if dx > 0 else 1]
             else:
-                src = p_hbm.at[:, pl.ds(N - 1 if dy > 0 else 0, 1), :]
-                dst = pb.at[pl.ds(1, N), pl.ds(3 if dy > 0 else 4 + N, 1), :]
+                src = p_hbm.at[:, N - 1 if dy > 0 else 0, :]
+                dst = hy.at[0 if dy > 0 else 1]
         else:
             at = 12 + DIRS.index(d)
             wide = 14 if dx == 0 or dy == 0 else 13
@@ -182,44 +180,82 @@
     own_x = list(range(XO, XO + N))
     load_l.wait()
     none = jnp.full((N, N), -1, jnp.int32)
+    lt[...] = jnp.full((NYF, DEPTH), -1, jnp.int32)
     lt[pl.ds(20, N), :] = tags(jnp.concatenate([none, lb[1, pl.ds(N, N), :], none], axis=0))
     coefficients(own_x, 16, 40)
+
+    def vertical(weight, value):
+        return weight * pltpu.roll(value, DEPTH - 1, 1) + pltpu.roll(weight * value, 1, 1)
+
+    zero = jnp.zeros((N, DEPTH), jnp.float32)
+    pb[0, pl.ds(4, N), :] = zero
+    pb[N + 1, pl.ds(4, N), :] = zero
+    s_ref[XO - 1, pl.ds(YO, N), :] = zero
+    s_ref[XO + N, pl.ds(YO, N), :] = zero
+    own = pl.ds(YO, N)
+    load_p.wait()
+    load_s.wait()
+    pb[pl.ds(1, N), 3, :] = zero
+    pb[pl.ds(1, N), 4 + N, :] = zero
+
+    @pl.loop(0, N // 2)
+    def _(i):
+        out = []
+        for x in (2 * i, 2 * i + 1):
+            fx = x + XO
+            s = s_ref[fx, own, :]
+            sn = [s_ref[fx - 1, own, :], s_ref[fx + 1, own, :],
+                  s_ref[fx, pl.ds(YO - 1, N), :], s_ref[fx, pl.ds(YO + 1, N), :]]
+            p = pb[x + 1, pl.ds(4, N), :]
+            pn = [pb[x, pl.ds(4, N), :], pb[x + 2, pl.ds(4, N), :],
+                  pb[x + 1, pl.ds(3, N), :], pb[x + 1, pl.ds(5, N), :]]
+            flow = (s + sn[0]) * (p - pn[0])
+            for n in range(1, 4):
+                flow = flow + (s + sn[n]) * (p - pn[n])
+            both = k_ref[fx, own, :] - 4.0 * s
+            flow = flow + (both * p - vertical(w_ref[fx, own, :], p))
+            out.append(sb[x] - flow)
+        for n in (0, 1):
+            rb[2 * i + n + XO, own, :] = out[n]
 
     arrive(0, DIRS)
     lt[pl.ds(0, 20), :] = tags(lb[0])[12:]
     lt[pl.ds(20, N), :] = tags(lb[1])
     lt[pl.ds(52, 20), :] = tags(lb[2])[:20]
 
-    def vertical(weight, value):
-        return weight * pltpu.roll(value, DEPTH - 1, 1) + pltpu.roll(weight * value, 1, 1)
-
-    for part in (range(0, XO), range(XO + N, NXF)):
+    coefficients([XO - 1, XO + N], 16, 40)
+    coefficients(own_x, 16, 8)
+    coefficients(own_x, 48, 8)
+
+    def outward(s, sn, p, pn):
+        return (s + sn) * (p - pn) - s * p
+
+    for d in SIDES:
+        @pl.when(there(d))
+        def _():
+            dx, dy = d
+            message(1, back(d)).wait_recv()
+            if dx:
+                f = XO if dx < 0 else XO + N - 1
+                rb[f, own, :] = rb[f, own, :] - outward(
+                    s_ref[f, own, :], s_ref[f + dx, own, :],
+                    pb[f - XO + 1, pl.ds(4, N), :], hx[0 if dx < 0 else 1])
+            else:
+                f = YO if dy < 0 else YO + N - 1
+                xs = pl.ds(XO, N)
+                rb[xs, f, :] = rb[xs, f, :] - outward(
+                    s_ref[xs, f, :], s_ref[xs, f + dy, :],
+                    pb[pl.ds(1, N), f - YO + 4, :], hy[0 if dy < 0 else 1])
+
+    start(2, [(0, -1), (0, 1), (-1, -1), (-1, 1), (1, -1), (1, 1), (-1, 0), (1, 0)])
+
+    for part in (range(0, XO - 1), range(XO + N + 1, NXF)):
         coefficients(list(part), 0, NYF)
-    coefficients(own_x, 0, 24)
-    coefficients(own_x, 48, 24)
-
-    load_p.wait()
-    load_s.wait()
-    arrive(1, SIDES)
-
-    @pl.loop(0, N)
-    def _(x):
-        fx = x + XO
-        own = pl.ds(YO, N)
-        s = s_ref[fx, own, :]
-        sn = [s_ref[fx - 1, own, :], s_ref[fx + 1, own, :],
-              s_ref[fx, pl.ds(YO - 1, N), :], s_ref[fx, pl.ds(YO + 1, N), :]]
-        p = pb[x + 1, pl.ds(4, N), :]
-        pn = [pb[x, pl.ds(4, N), :], pb[x + 2, pl.ds(4, N), :],
-              pb[x + 1, pl.ds(3, N), :], pb[x + 1, pl.ds(5, N), :]]
-        flow = (s + sn[0]) * (p - pn[0])
-        for i in range(1, 4):
-            flow = flow + (s + sn[i]) * (p - pn[i])
-        both = k_ref[fx, own, :] - 4.0 * s
-        flow = flow + (both * p - vertical(w_ref[fx, own, :], p))
-        rb[fx, own, :] = sb[x] - flow
-
-    start(2, DIRS)
+    coefficients([XO - 1, XO + N], 0, 16)
+    coefficients([XO - 1, XO + N], 56, 16)
+    coefficients(own_x, 0, 16)
+    coefficients(own_x, 56, 16)
+
     @pl.loop(4, NXF - 4)
     def _(x):
         at = pl.ds(4, 64)
@@ -253,35 +289,37 @@
             ua[x, at, :] = u
             pa[x, at, :] = s_ref[x, at, :] * u
 
-    def sweep(first, u_in, p_in, u_out, p_out, base):
+    def sweep(rows, first, u_in, p_in, u_out, p_out, base):
         y0, ny = first, NYF - 2 * first
         at = pl.ds(y0, ny)
         lo = pl.ds(y0 - 4, ny)
         hi_ = pl.ds(y0 + 4, ny)
 
-        def row(x):
+        def column(x):
+            return vertical(w_ref[x, at, :], u_in[x, at, :])
+
+        def row(x, column):
             s = s_ref[x, at, :]
             u = u_in[x, at, :]
             un = (u_in[x - 4, at, :] + u_in[x + 4, at, :]
                   + u_in[x, lo, :] + u_in[x, hi_, :])
             pn = (p_in[x - 4, at, :] + p_in[x + 4, at, :]
                   + p_in[x, lo, :] + p_in[x, hi_, :])
-            total = s * un + pn + vertical(w_ref[x, at, :], u)
-            new = base[x, at, :] + 0.2 * u + k_ref[x, at, :] * total
+            new = base[x, at, :] + 0.2 * u + k_ref[x, at, :] * (s * un + pn + column)
             return s, new
 
-        @pl.loop(0, (NXF - 2 * first) // 2)
+        @pl.loop(0, pl.cdiv(NXF - 2 * first, rows))
         def _(i):
-            xs = (first + 2 * i, first + 2 * i + 1)
-            out = [row(x) for x in xs]
-            for x, (s, new) in zip(xs, out):
-                u_out[x, at, :] = new
+            x0 = first + rows * i
+            out = [row(x0 + n, column(x0 + n)) for n in range(rows)]
+            for n, (s, new) in enumerate(out):
+                u_out[x0 + n, at, :] = new
                 if p_out is not None:
-                    p_out[x, at, :] = s * new
-
-    sweep(8, ua, pa, ub, qb, ua)
-    sweep(12, ub, qb, uc, pa, ua)
-    sweep(16, uc, pa, ub, None, ua)
+                    p_out[x0 + n, at, :] = s * new
+
+    sweep(R1, 8, ua, pa, ub, qb, ua)
+    sweep(R2, 12, ub, qb, uc, pa, ua)
+    sweep(R3, 16, uc, pa, ub, None, ua)
 
     @pl.loop(0, N)
     def _(x):
@@ -313,6 +351,8 @@
             pltpu.VMEM((16, DEPTH), jnp.float32),
             pltpu.VMEM((3, 3 * N, N), jnp.int32),
             pltpu.VMEM((NYF, DEPTH), jnp.int32),
+            pltpu.VMEM((2, N, DEPTH), jnp.float32),
+            pltpu.VMEM((2, N, DEPTH), jnp.float32),
             pltpu.SemaphoreType.DMA((20,)),
             pltpu.SemaphoreType.DMA((20,)),
             pltpu.SemaphoreType.DMA((4,)),

time: 41.6 us -> 36 us (0.87)
  the two profiles are of different devices: /device:TPU:31 before, /device:TPU:3 now
where the time goes in v3:
time: 36 us; the launch traced here: 35.9 us
  Pallas kernels  35.3 us (98%)
  between operations  0.64 us (2%)
    pallas_call x1, Pallas kernels, per_device(): pl.pallas_call(exchange, out_shape=(field,) * 4, in_specs=[hbm] * 4, out_...  29.6 us
    pallas_call x1, Pallas kernels, per_device(): pl.pallas_call(relax, out_shape=(own, own), in_specs=[vmem] * 4, out_spec...  5.71 us

profile of v3, /device:TPU:3, one launch (start us, length us, event | category | flops | bytes accessed | tf_op | source)
XLA Modules:
  0.0 35.9 jit_solution(16081804898502284362)
XLA Ops:
  0.6 29.6 %exchange.1 = (f32[66,72,128]{2,1,0:T(8,128)S(1)}, f32[66,72,128]{2,1,0:T(8,128)S(1)}, f32[66,72,128]{2,1,0:T(8,128)S(1)}, f32[66,72,128]{2,1,0:T(8,128)S(1)}) custom-call(f32[32,32,128]{2,1,0:T(8,128)} %p_hbm.1, f32[32,32,128]{2,1,0:T(8,128)} %src_hbm.1, s32[32,32]{1,0:T(8,128)} %lab_hbm.1, f32[16,128]{1,0:T(8,128)} %tab_hbm.1), custom_call_target="tpu_custom_call" | custom-call | tf_op jit(solution)/shard_map/exchange/pallas_call | solution.py:343
  30.2 5.7 %relax.1 = (f32[32,32,128]{2,1,0:T(8,128)}, f32[32,32,128]{2,1,0:T(8,128)}) custom-call(f32[66,72,128]{2,1,0:T(8,128)S(1)} %get-tuple-element.6.s_ref, f32[66,72,128]{2,1,0:T(8,128)S(1)} %get-tuple-element.7.w_ref, f32[66,72,128]{2,1,0:T(8,128)S(1)} %get-tuple-element.8.k_ref, f32[66,72,128]{2,1,0:T(8,128)S(1)} %get-tuple-element.9.rb), custom_call_target="tpu_custom_call" | custom-call | tf_op jit(solution)/shard_map/relax/pallas_call | solution.py:365

commit v4 on v3

--- a/solution.py
+++ b/solution.py
@@ -10,17 +10,37 @@
 DEPTH = 128
 XO, YO = 17, 20
 NXF, NYF = 66, 72
-R1, R2, R3 = 10, 7, 7
+R1, R2, R3 = 50, 42, 34
 DIRS = [(dx, dy) for dx in (-1, 0, 1) for dy in (-1, 0, 1) if (dx, dy) != (0, 0)]
+ORDER = [(0, -1), (0, 1), (-1, 0), (1, 0), (-1, -1), (-1, 1), (1, -1), (1, 1)]
 SIDES = [(-1, 0), (1, 0), (0, -1), (0, 1)]
 
 
-def span(step, width, origin):
+def pieces(d, edge):
+    dx, dy = d
+    if dy == 0:
+        if not edge:
+            return [((2, 14), (1, N - 2))]
+        return [((1, 1), (0, N - 1)), ((2, 14), (0, 0)), ((2, 14), (N - 1, N - 1))]
+    if dx == 0:
+        if not edge:
+            return [((1, N - 2), (2, 14))]
+        return [((0, N - 1), (1, 1)), ((0, 0), (2, 14)), ((N - 1, N - 1), (2, 14))]
+    if not edge:
+        return [((2, 6), (2, 12)), ((7, 12), (2, 6))]
+    return [((1, 1), (1, 13)), ((2, 13), (1, 1))]
+
+
+def span(step, lo, hi):
     if step == 1:
-        return origin + N - width, origin - width
+        return N - hi, hi - lo + 1
     if step == -1:
-        return origin, origin + N
-    return origin, origin
+        return lo - 1, hi - lo + 1
+    return lo, hi - lo + 1
+
+
+PARTS = [(d, edge, n) for edge in (False, True) for d in DIRS for n in range(len(pieces(d, edge)))]
+COPIES = 12 + len(PARTS)
 
 
 def exchange(p_hbm, src_hbm, lab_hbm, tab_hbm, s_ref, w_ref, k_ref, rb,
@@ -92,53 +112,60 @@
 
     pl.semaphore_wait(barrier, count)
 
-    def message(kind, d):
-        dx, dy = d
-        if kind == 0:
-            at = DIRS.index(d)
-            src = lab_hbm
-            dst = lb.at[1 - dy, pl.ds(N * (1 - dx), N), :]
-        elif kind == 1:
-            at = 8 + SIDES.index(d)
-            if dx:
-                src = p_hbm.at[N - 1 if dx > 0 else 0]
-                dst = hx.at[0 if dx > 0 else 1]
-            else:
-                src = p_hbm.at[:, N - 1 if dy > 0 else 0, :]
-                dst = hy.at[0 if dy > 0 else 1]
-        else:
-            at = 12 + DIRS.index(d)
-            wide = 14 if dx == 0 or dy == 0 else 13
-            sx, tx = span(dx, wide, XO)
-            sy, ty = span(dy, wide, YO)
-            nx = wide if dx else N
-            ny = wide if dy else N
-            src = rb.at[pl.ds(sx, nx), pl.ds(sy, ny), :]
-            dst = rb.at[pl.ds(tx, nx), pl.ds(ty, ny), :]
+    def remote(src, dst, at, d):
         return pltpu.make_async_remote_copy(
             src_ref=src, dst_ref=dst, send_sem=send.at[at], recv_sem=recv.at[at],
             device_id=device(d), device_id_type=MESH)
 
-    def start(kind, dirs):
+    def messages(kind, d):
+        dx, dy = d
+        if kind == 0:
+            r0, rows = (15, 17) if dx > 0 else (0, 17) if dx < 0 else (0, N)
+            return [remote(lab_hbm.at[pl.ds(r0, rows), :],
+                           lb.at[1 - dy, pl.ds(N * (1 - dx) + r0, rows), :], DIRS.index(d), d)]
+        if kind == 1:
+            at = 8 + SIDES.index(d)
+            if dx:
+                return [remote(p_hbm.at[N - 1 if dx > 0 else 0], hx.at[0 if dx > 0 else 1], at, d)]
+            return [remote(p_hbm.at[:, N - 1 if dy > 0 else 0, :], hy.at[0 if dy > 0 else 1], at, d)]
+        edge = kind == 3
+        out = []
+        for n, (rows, cols) in enumerate(pieces(d, edge)):
+            x, nx = span(dx, *rows)
+            y, ny = span(dy, *cols)
+            x = x + XO
+            y = y + YO
+            out.append(remote(rb.at[pl.ds(x, nx), pl.ds(y, ny), :],
+                              rb.at[pl.ds(x - N * dx, nx), pl.ds(y - N * dy, ny), :],
+                              12 + PARTS.index((d, edge, n)), d))
+        return out
+
+    def start(kinds, dirs):
         for d in dirs:
             @pl.when(there(d))
             def _():
-                message(kind, d).start()
-
-    def arrive(kind, dirs):
+                for kind in kinds:
+                    for m in messages(kind, d):
+                        m.start()
+
+    def arrive(kinds, dirs):
         for d in dirs:
             @pl.when(there(back(d)))
             def _():
-                message(kind, d).wait_recv()
-
-    def sent(kind, dirs):
+                for kind in kinds:
+                    for m in messages(kind, d):
+                        m.wait_recv()
+
+    def sent(kinds, dirs):
         for d in dirs:
             @pl.when(there(d))
             def _():
-                message(kind, d).wait_send()
-
-    start(1, SIDES)
-    start(0, DIRS)
+                for kind in kinds:
+                    for m in messages(kind, d):
+                        m.wait_send()
+
+    start([1], SIDES)
+    start([0], DIRS)
 
     load_t.wait()
     half = 0.5 * tb[...]
@@ -198,10 +225,10 @@
     pb[pl.ds(1, N), 3, :] = zero
     pb[pl.ds(1, N), 4 + N, :] = zero
 
-    @pl.loop(0, N // 2)
+    @pl.loop(0, N // 8)
     def _(i):
         out = []
-        for x in (2 * i, 2 * i + 1):
+        for x in [8 * i + n for n in range(8)]:
             fx = x + XO
             s = s_ref[fx, own, :]
             sn = [s_ref[fx - 1, own, :], s_ref[fx + 1, own, :],
@@ -215,10 +242,11 @@
             both = k_ref[fx, own, :] - 4.0 * s
             flow = flow + (both * p - vertical(w_ref[fx, own, :], p))
             out.append(sb[x] - flow)
-        for n in (0, 1):
-            rb[2 * i + n + XO, own, :] = out[n]
-
-    arrive(0, DIRS)
+        for n in range(8):
+            rb[8 * i + n + XO, own, :] = out[n]
+
+    start([2], ORDER)
+    arrive([0], DIRS)
     lt[pl.ds(0, 20), :] = tags(lb[0])[12:]
     lt[pl.ds(20, N), :] = tags(lb[1])
     lt[pl.ds(52, 20), :] = tags(lb[2])[:20]
@@ -234,7 +262,7 @@
         @pl.when(there(d))
         def _():
             dx, dy = d
-            message(1, back(d)).wait_recv()
+            messages(1, back(d))[0].wait_recv()
             if dx:
                 f = XO if dx < 0 else XO + N - 1
                 rb[f, own, :] = rb[f, own, :] - outward(
@@ -247,7 +275,7 @@
                     s_ref[xs, f, :], s_ref[xs, f + dy, :],
                     pb[pl.ds(1, N), f - YO + 4, :], hy[0 if dy < 0 else 1])
 
-    start(2, [(0, -1), (0, 1), (-1, -1), (-1, 1), (1, -1), (1, 1), (-1, 0), (1, 0)])
+    start([3], ORDER)
 
     for part in (range(0, XO - 1), range(XO + N + 1, NXF)):
         coefficients(list(part), 0, NYF)
@@ -264,11 +292,10 @@
                 + (s_ref[x, pl.ds(0, 64), :] + s_ref[x, pl.ds(8, 64), :]))
         k_ref[x, at, :] = jnp.where(s > 0.0, 0.8 / diag, 0.0)
 
-    arrive(2, DIRS)
-
-    sent(0, DIRS)
-    sent(1, SIDES)
-    sent(2, DIRS)
+    arrive([2, 3], DIRS)
+
+    sent([1], SIDES)
+    sent([0, 2, 3], DIRS)
 
 
 def relax(s_ref, w_ref, k_ref, rb, res_hbm, cor_hbm, ua, pa, ub, qb, uc, ob, local):
@@ -321,18 +348,23 @@
     sweep(R2, 12, ub, qb, uc, pa, ua)
     sweep(R3, 16, uc, pa, ub, None, ua)
 
-    @pl.loop(0, N)
-    def _(x):
-        fx = x + XO
-        at = pl.ds(YO, N)
-        ob[x] = (0.5 * ub[fx, at, :]
-                 + 0.125 * (ub[fx - 1, at, :] + ub[fx + 1, at, :]
-                            + ub[fx, pl.ds(YO - 1, N), :] + ub[fx, pl.ds(YO + 1, N), :]))
-
-    out_c = pltpu.make_async_copy(ob, cor_hbm, local.at[1])
-    out_c.start()
+    def out_c(c):
+        rows = pl.ds(8 * c, 8)
+        return pltpu.make_async_copy(ob.at[rows], cor_hbm.at[rows], local.at[1 + c])
+
+    for c in range(4):
+        @pl.loop(8 * c, 8 * c + 8, unroll=True)
+        def _(x):
+            fx = x + XO
+            at = pl.ds(YO, N)
+            ob[x] = (0.5 * ub[fx, at, :]
+                     + 0.125 * (ub[fx - 1, at, :] + ub[fx + 1, at, :]
+                                + ub[fx, pl.ds(YO - 1, N), :] + ub[fx, pl.ds(YO + 1, N), :]))
+
+        out_c(c).start()
     out_r.wait()
-    out_c.wait()
+    for c in range(4):
+        out_c(c).wait()
 
 
 def per_device(pressure, source, labels, region_table):
@@ -353,8 +385,8 @@
             pltpu.VMEM((NYF, DEPTH), jnp.int32),
             pltpu.VMEM((2, N, DEPTH), jnp.float32),
             pltpu.VMEM((2, N, DEPTH), jnp.float32),
-            pltpu.SemaphoreType.DMA((20,)),
-            pltpu.SemaphoreType.DMA((20,)),
+            pltpu.SemaphoreType.DMA((COPIES,)),
+            pltpu.SemaphoreType.DMA((COPIES,)),
             pltpu.SemaphoreType.DMA((4,)),
         ],
         compiler_params=pltpu.CompilerParams(
@@ -369,7 +401,7 @@
         out_specs=(hbm, hbm),
         scratch_shapes=[field] * 5 + [
             pltpu.VMEM((N, N, DEPTH), jnp.float32),
-            pltpu.SemaphoreType.DMA((2,)),
+            pltpu.SemaphoreType.DMA((5,)),
         ],
         compiler_params=pltpu.CompilerParams(vmem_limit_bytes=24 << 20),
         name="relax",

time: 36 us -> 29.5 us (0.82)
  the two profiles are of different devices: /device:TPU:3 before, /device:TPU:6 now
where the time goes in v4:
time: 29.5 us; the launch traced here: 29.4 us
  Pallas kernels  28.7 us (97%)
  between operations  0.64 us (2%)
    pallas_call x1, Pallas kernels, per_device(): pl.pallas_call(exchange, out_shape=(field,) * 4, in_specs=[hbm] * 4, out_...  24.6 us
    pallas_call x1, Pallas kernels, per_device(): pl.pallas_call(relax, out_shape=(own, own), in_specs=[vmem] * 4, out_spec...  4.18 us

profile of v4, /device:TPU:6, one launch (start us, length us, event | category | flops | bytes accessed | tf_op | source)
XLA Modules:
  0.0 29.4 jit_solution(6496880903505209324)
XLA Ops:
  0.6 24.6 %exchange.1 = (f32[66,72,128]{2,1,0:T(8,128)S(1)}, f32[66,72,128]{2,1,0:T(8,128)S(1)}, f32[66,72,128]{2,1,0:T(8,128)S(1)}, f32[66,72,128]{2,1,0:T(8,128)S(1)}) custom-call(f32[32,32,128]{2,1,0:T(8,128)} %p_hbm.1, f32[32,32,128]{2,1,0:T(8,128)} %src_hbm.1, s32[32,32]{1,0:T(8,128)} %lab_hbm.1, f32[16,128]{1,0:T(8,128)} %tab_hbm.1), custom_call_target="tpu_custom_call" | custom-call | tf_op jit(solution)/shard_map/exchange/pallas_call | solution.py:375
  25.2 4.2 %relax.1 = (f32[32,32,128]{2,1,0:T(8,128)}, f32[32,32,128]{2,1,0:T(8,128)}) custom-call(f32[66,72,128]{2,1,0:T(8,128)S(1)} %get-tuple-element.6.s_ref, f32[66,72,128]{2,1,0:T(8,128)S(1)} %get-tuple-element.7.w_ref, f32[66,72,128]{2,1,0:T(8,128)S(1)} %get-tuple-element.8.k_ref, f32[66,72,128]{2,1,0:T(8,128)S(1)} %get-tuple-element.9.rb), custom_call_target="tpu_custom_call" | custom-call | tf_op jit(solution)/shard_map/relax/pallas_call | solution.py:397

commit v5 on v4

v5 whole, which is shorter than its diff:
```python
import jax
import jax.numpy as jnp
from jax import lax
from jax.experimental import pallas as pl
from jax.experimental.pallas import tpu as pltpu
from jax.sharding import PartitionSpec as P

MESH = pl.DeviceIdType.MESH
N = 32
DEPTH = 128
XO, YO = 17, 20
NXF, NYF = 66, 72
DIRS = [(dx, dy) for dx in (-1, 0, 1) for dy in (-1, 0, 1) if (dx, dy) != (0, 0)]
ORDER = [(0, -1), (0, 1), (-1, -1), (-1, 1), (1, -1), (1, 1), (-1, 0), (1, 0)]
DIRS_X, DIRS_Y = [(-1, 0), (1, 0)], [(0, -1), (0, 1)]
DIRS_XY = [(-1, -1), (-1, 1), (1, -1), (1, 1)]
SIDES = DIRS_X + DIRS_Y


def pieces(d, stage):
    dx, dy = d
    if dy == 0:
        return [((1, 14), (1, N - 2))] if stage == (dx > 0) else []
    if dx == 0:
        return [((1, 15), (1, 14)) if stage == 0 else ((16, N - 2), (1, 14))]
    return [((2, 6), (2, 12)), ((7, 12), (2, 6))] if stage == (dx > 0) else []


def span(step, lo, hi):
    if step == 1:
        return N - hi, hi - lo + 1
    if step == -1:
        return lo - 1, hi - lo + 1
    return lo, hi - lo + 1


XSIDES, YSIDES, CORNERS = DIRS_X, DIRS_Y, DIRS_XY
KINDS = {0: DIRS, 1: SIDES, 2: DIRS, 3: DIRS, 4: YSIDES, 5: XSIDES, 6: CORNERS}
KEYS = [(kind, d, n) for kind, dirs in KINDS.items() for d in dirs
        for n in range(len(pieces(d, kind - 2)) if kind in (2, 3) else (1, 1, 0, 0, 2, 2, 3)[kind])]


def columns(reach, x):
    beyond = max(XO - x, x - (XO + N - 1), 1)
    side = reach - 4 * (-(-(beyond - 1) // 4))
    return YO - side - 3, -(-(N + 2 * side) // 8) * 8


def exchange(p_hbm, src_hbm, lab_hbm, tab_hbm, s_ref, w_ref, k_ref, rb,
             pb, sb, tb, lb, lt, hx, hy, ax, ay, bx, by, rx, cy, cc,
             send, recv, local):
    groups = lax.axis_size("group")
    spaces = lax.axis_size("space")
    gi = lax.axis_index("group")
    si = lax.axis_index("space")

    def there(d):
        dx, dy = d
        ok = None
        if dx == 1:
            ok = si < spaces - 1
        elif dx == -1:
            ok = si > 0
        if dy:
            okg = gi < groups - 1 if dy == 1 else gi > 0
            ok = okg if ok is None else jnp.logical_and(ok, okg)
        return ok

    def back(d):
        return (-d[0], -d[1])

    def device(d):
        return (gi + d[1], si + d[0])

    halves = ((0, 17), (17, 15))
    load_p = [pltpu.make_async_copy(p_hbm.at[pl.ds(a, n)], pb.at[pl.ds(1 + a, n), pl.ds(4, N), :],
                                    local.at[4 + h]) for h, (a, n) in enumerate(halves)]
    load_s = [pltpu.make_async_copy(src_hbm.at[pl.ds(a, n)], sb.at[pl.ds(a, n)],
                                    local.at[h]) for h, (a, n) in enumerate(halves)]
    load_l = pltpu.make_async_copy(lab_hbm, lb.at[1, pl.ds(N, N), :], local.at[2])
    load_t = pltpu.make_async_copy(tab_hbm, tb, local.at[3])
    load_l.start()
    load_t.start()
    for h in (0, 1):
        load_p[h].start()
        load_s[h].start()

    barrier = pltpu.get_barrier_semaphore()
    count = jnp.int32(0)
    for d in DIRS:
        ok = there(d)
        count = count + ok.astype(jnp.int32)

        @pl.when(ok)
        def _():
            pl.semaphore_signal(barrier, 1, device_id=device(d), device_id_type=MESH)

    for d in DIRS:
        @pl.when(jnp.logical_not(there(d)))
        def _():
            dx, dy = d
            lb[1 + dy, pl.ds(N * (1 + dx), N), :] = jnp.full((N, N), -1, jnp.int32)

    for d in SIDES:
        @pl.when(jnp.logical_not(there(d)))
        def _():
            dx, dy = d
            if dx:
                hx[int(dx > 0)] = jnp.zeros((N, DEPTH), jnp.float32)
                r0 = XO - 14 if dx < 0 else XO + N

                @pl.loop(0, 14)
                def _(i):
                    rb[r0 + i] = jnp.zeros((NYF, DEPTH), jnp.float32)
            else:
                hy[int(dy > 0)] = jnp.zeros((N, DEPTH), jnp.float32)
                c0 = YO - 14 if dy < 0 else YO + N

                @pl.loop(XO - 14, XO + N + 14)
                def _(i):
                    rb[i, pl.ds(c0, 14), :] = jnp.zeros((14, DEPTH), jnp.float32)

    def messages(kind, d):
        dx, dy = d
        ex, ey = int(dx > 0), int(dy > 0)
        last = N - 1
        if kind == 0:
            r0, rows = (15, 17) if dx > 0 else (0, 17) if dx < 0 else (0, N)
            ends = [(lab_hbm.at[pl.ds(r0, rows), :],
                     lb.at[1 - dy, pl.ds(N * (1 - dx) + r0, rows), :])]
        elif kind == 1:
            ends = [(p_hbm.at[last * ex], hx.at[1 - ex]) if dx
                    else (p_hbm.at[:, last * ey, :], hy.at[1 - ey])]
        elif kind in (2, 3):
            ends = []
            for rows, cols in pieces(d, kind - 2):
                x, nx = span(dx, *rows)
                y, ny = span(dy, *cols)
                x = x + XO
                y = y + YO
                ends.append((rb.at[pl.ds(x, nx), pl.ds(y, ny), :],
                             rb.at[pl.ds(x - N * dx, nx), pl.ds(y - N * dy, ny), :]))
        elif kind == 4:
            y = (N - 14) * ey
            ends = [(rx.at[e, pl.ds(y, 14), :],
                     rb.at[XO + last * e, pl.ds(YO + y - N * dy, 14), :]) for e in (0, 1)]
        elif kind == 5:
            x = (N - 14) * ex
            ends = [(cy.at[e, pl.ds(x, 14), :],
                     rb.at[pl.ds(XO + x - N * dx, 14), YO + last * e, :]) for e in (0, 1)]
        else:
            x, y = (N - 13 if ex else 1), (N - 13 if ey else 1)
            fx, fy = XO + last * ex - N * dx, YO + last * ey - N * dy
            ends = [(rx.at[ex, pl.ds(y, 12), :], rb.at[fx, pl.ds(YO + y - N * dy, 12), :]),
                    (cy.at[ey, pl.ds(x, 12), :], rb.at[pl.ds(XO + x - N * dx, 12), fy, :]),
                    (cc.at[2 * ex + ey], rb.at[fx, pl.ds(fy, 1), :])]
        return [pltpu.make_async_remote_copy(
            src_ref=src, dst_ref=dst, send_sem=send.at[KEYS.index((kind, d, n))],
            recv_sem=recv.at[KEYS.index((kind, d, n))], device_id=device(d), device_id_type=MESH)
            for n, (src, dst) in enumerate(ends)]

    def held(kinds, d):
        return [k for k in kinds if any(key[:2] == (k, d) for key in KEYS)]

    def start(kinds, dirs):
        for d in dirs:
            if not held(kinds, d):
                continue

            @pl.when(there(d))
            def _():
                for kind in held(kinds, d):
                    for m in messages(kind, d):
                        m.start()

    def arrive(kinds, dirs):
        for d in dirs:
            @pl.when(there(back(d)))
            def _():
                for kind in held(kinds, d):
                    for m in messages(kind, d):
                        m.wait_recv()

    def sent(kinds, dirs):
        for d in dirs:
            @pl.when(there(d))
            def _():
                for kind in held(kinds, d):
                    for m in messages(kind, d):
                        m.wait_send()


    load_t.wait()
    half = 0.5 * tb[...]
    lane = lax.broadcasted_iota(jnp.int32, (16, DEPTH), 1)
    up = jnp.where(lane < DEPTH - 1, pltpu.roll(half, DEPTH - 1, 1), 0.0)
    down = jnp.where(lane > 0, pltpu.roll(half, 1, 1), 0.0)
    wup = jnp.where(lane < DEPTH - 1, half + up, 0.0)
    vert = 6.0 * half + (up + down)
    wide = jnp.concatenate([half, wup, vert], axis=1)
    hi = wide.astype(jnp.bfloat16)
    rest = wide - hi.astype(jnp.float32)
    mid = rest.astype(jnp.bfloat16)
    low = (rest - mid.astype(jnp.float32)).astype(jnp.bfloat16)
    table = jnp.concatenate(
        [hi, mid, low, jnp.zeros((DEPTH - 48, 3 * DEPTH), jnp.bfloat16)], axis=0)

    def tags(block):
        pad = jnp.full((N, DEPTH - 3 * N), -1, jnp.int32)
        return jnp.concatenate([block.T, pad], axis=1)

    def coefficients(xs, y0, ny):
        lanes = lax.broadcasted_iota(jnp.int32, (ny, DEPTH), 1)
        slot = jnp.where(lanes < 48, lanes & 15, -9)
        at = pl.ds(y0, ny)
        tag = lt[at, :]
        hits = []
        for x in xs:
            c = x + N - XO
            hit = jnp.broadcast_to(tag[:, c:c + 1], (ny, DEPTH)) == slot
            hits.append(jnp.where(hit, 1.0, 0.0))
        onehot = jnp.concatenate(hits, axis=0).astype(jnp.bfloat16)
        out = jnp.dot(onehot, table, preferred_element_type=jnp.float32)
        for n, x in enumerate(xs):
            part = out[n * ny:(n + 1) * ny]
            s_ref[x, at, :] = part[:, :DEPTH]
            w_ref[x, at, :] = part[:, DEPTH:2 * DEPTH]
            k_ref[x, at, :] = part[:, 2 * DEPTH:]

    own_x = list(range(XO, XO + N))
    load_l.wait()
    none = jnp.full((N, N), -1, jnp.int32)
    lt[...] = jnp.full((NYF, DEPTH), -1, jnp.int32)
    lt[pl.ds(20, N), :] = tags(jnp.concatenate([none, lb[1, pl.ds(N, N), :], none], axis=0))

    def vertical(weight, value):
        return weight * pltpu.roll(value, DEPTH - 1, 1) + pltpu.roll(weight * value, 1, 1)

    zero = jnp.zeros((N, DEPTH), jnp.float32)
    pb[0, pl.ds(4, N), :] = zero
    pb[N + 1, pl.ds(4, N), :] = zero
    s_ref[XO - 1, pl.ds(YO, N), :] = zero
    s_ref[XO + N, pl.ds(YO, N), :] = zero
    own = pl.ds(YO, N)
    for h, (a, n) in enumerate(halves):
        coefficients(own_x[a:a + n], 16, 40)
        load_p[h].wait()
        load_s[h].wait()
        pb[pl.ds(1 + a, n), 3, :] = zero[:n]
        pb[pl.ds(1 + a, n), 4 + N, :] = zero[:n]

        @pl.loop(2 * h, 2 * h + 2)
        def _(i):
            out = []
            for x in [8 * i + n for n in range(8)]:
                fx = x + XO
                s = s_ref[fx, own, :]
                sn = [s_ref[fx - 1, own, :], s_ref[fx + 1, own, :],
                      s_ref[fx, pl.ds(YO - 1, N), :], s_ref[fx, pl.ds(YO + 1, N), :]]
                p = pb[x + 1, pl.ds(4, N), :]
                pn = [pb[x, pl.ds(4, N), :], pb[x + 2, pl.ds(4, N), :],
                      pb[x + 1, pl.ds(3, N), :], pb[x + 1, pl.ds(5, N), :]]
                flow = (s + sn[0]) * (p - pn[0])
                for n in range(1, 4):
                    flow = flow + (s + sn[n]) * (p - pn[n])
                both = k_ref[fx, own, :] - 4.0 * s
                flow = flow + (both * p - vertical(w_ref[fx, own, :], p))
                out.append(sb[x] - flow)
            for n in range(8):
                rb[8 * i + n + XO, own, :] = out[n]

        if h == 0:
            pl.semaphore_wait(barrier, count)
            start([1], SIDES)
            start([0], DIRS)
        start([2 + h], ORDER)

    def outward(s, sn, p, pn):
        return (s + sn) * (p - pn) - s * p

    arrive([0, 1], XSIDES)
    lt[pl.ds(20, N), :] = tags(lb[1])
    coefficients([XO - 1, XO + N], 16, 40)
    for e, (f, g) in enumerate(((XO, XO - 1), (XO + N - 1, XO + N))):
        s, sn = s_ref[f, own, :], s_ref[g, own, :]
        p, pn = pb[f - XO + 1, pl.ds(4, N), :], hx[e]
        delta = outward(s, sn, p, pn)
        ax[e] = delta
        bx[e] = outward(sn, s, pn, p)
        rx[e] = rb[f, own, :] - delta
    start([4], YSIDES)

    arrive([0, 1], YSIDES)
    lt[pl.ds(0, 20), :] = tags(jnp.concatenate([none, lb[0, pl.ds(N, N), :], none], axis=0))[12:]
    lt[pl.ds(52, 20), :] = tags(jnp.concatenate([none, lb[2, pl.ds(N, N), :], none], axis=0))[:20]
    coefficients(own_x, 16, 8)
    coefficients(own_x, 48, 8)
    rows = pl.ds(XO, N)
    for e, (f, g) in enumerate(((YO, YO - 1), (YO + N - 1, YO + N))):
        s, sn = s_ref[rows, f, :], s_ref[rows, g, :]
        p, pn = pb[pl.ds(1, N), f - YO + 4, :], hy[e]
        delta = outward(s, sn, p, pn)
        ay[e] = delta
        by[e] = outward(sn, s, pn, p)
        cy[e] = rb[rows, f, :] - delta
    for ex in (0, 1):
        for ey in (0, 1):
            cc[2 * ex + ey] = (rx[ex, pl.ds((N - 1) * ey, 1), :]
                               - ay[ey, pl.ds((N - 1) * ex, 1), :])
    start([5], XSIDES)
    start([6], CORNERS)

    arrive([0], CORNERS)
    lt[pl.ds(0, 20), :] = tags(lb[0])[12:]
    lt[pl.ds(52, 20), :] = tags(lb[2])[:20]
    for part in (range(0, XO - 1), range(XO + N + 1, NXF)):
        coefficients(list(part), 0, NYF)
    coefficients([XO - 1, XO + N], 0, 24)
    coefficients([XO - 1, XO + N], 48, 24)
    coefficients(own_x, 0, 16)
    coefficients(own_x, 56, 16)

    for x in range(XO - 13, XO + N + 13):
        y0, ny = columns(13, x)
        at = pl.ds(y0, ny)
        s = s_ref[x, at, :]
        diag = (k_ref[x, at, :] + (s_ref[x - 4, at, :] + s_ref[x + 4, at, :])
                + (s_ref[x, pl.ds(y0 - 4, ny), :] + s_ref[x, pl.ds(y0 + 4, ny), :]))
        k_ref[x, at, :] = jnp.where(s > 0.0, 0.8 / diag, 0.0)

    sent(list(KINDS), DIRS)
    for e, (f, g) in enumerate(((XO, XO - 1), (XO + N - 1, XO + N))):
        rb[f, own, :] = rb[f, own, :] - ax[e]
    for e, (f, g) in enumerate(((YO, YO - 1), (YO + N - 1, YO + N))):
        rb[rows, f, :] = rb[rows, f, :] - ay[e]
    arrive([2, 3, 4, 5, 6], ORDER)
    for e, g in enumerate((XO - 1, XO + N)):
        @pl.when(there(XSIDES[e]))
        def _():
            rb[g, own, :] = rb[g, own, :] - bx[e]
    for e, g in enumerate((YO - 1, YO + N)):
        @pl.when(there(YSIDES[e]))
        def _():
            rb[rows, g, :] = rb[rows, g, :] - by[e]


def relax(s_ref, w_ref, k_ref, rb, res_hbm, cor_hbm, ua, pa, ub, qb, uc, ob, local):
    out_r = pltpu.make_async_copy(rb.at[pl.ds(XO, N), pl.ds(YO, N), :], res_hbm, local.at[0])
    out_r.start()

    def vertical(weight, value):
        return weight * pltpu.roll(value, DEPTH - 1, 1) + pltpu.roll(weight * value, 1, 1)

    for x in range(XO - 13, XO + N + 13):
        y0, ny = columns(13, x)
        at = pl.ds(y0, ny)
        mean = (0.5 * rb[x, at, :]
                + 0.125 * (rb[x - 1, at, :] + rb[x + 1, at, :]
                           + rb[x, pl.ds(y0 - 1, ny), :] + rb[x, pl.ds(y0 + 1, ny), :]))
        u = k_ref[x, at, :] * mean
        ua[x, at, :] = u
        pa[x, at, :] = s_ref[x, at, :] * u

    def sweep(reach, u_in, p_in, u_out, p_out, base):
        for x in range(XO - reach, XO + N + reach):
            y0, ny = columns(reach, x)
            at = pl.ds(y0, ny)
            s = s_ref[x, at, :]
            u = u_in[x, at, :]
            un = (u_in[x - 4, at, :] + u_in[x + 4, at, :]
                  + u_in[x, pl.ds(y0 - 4, ny), :] + u_in[x, pl.ds(y0 + 4, ny), :])
            pn = (p_in[x - 4, at, :] + p_in[x + 4, at, :]
                  + p_in[x, pl.ds(y0 - 4, ny), :] + p_in[x, pl.ds(y0 + 4, ny), :])
            total = s * un + pn + vertical(w_ref[x, at, :], u)
            new = base[x, at, :] + 0.2 * u + k_ref[x, at, :] * total
            u_out[x, at, :] = new
            if p_out is not None:
                p_out[x, at, :] = s * new

    sweep(9, ua, pa, ub, qb, ua)
    sweep(5, ub, qb, uc, pa, ua)
    sweep(1, uc, pa, ub, None, ua)

    def out_c(c):
        rows = pl.ds(8 * c, 8)
        return pltpu.make_async_copy(ob.at[rows], cor_hbm.at[rows], local.at[1 + c])

    for c in range(4):
        @pl.loop(8 * c, 8 * c + 8, unroll=True)
        def _(x):
            fx = x + XO
            at = pl.ds(YO, N)
            ob[x] = (0.5 * ub[fx, at, :]
                     + 0.125 * (ub[fx - 1, at, :] + ub[fx + 1, at, :]
                                + ub[fx, pl.ds(YO - 1, N), :] + ub[fx, pl.ds(YO + 1, N), :]))

        out_c(c).start()
    out_r.wait()
    for c in range(4):
        out_c(c).wait()


def per_device(pressure, source, labels, region_table):
    hbm = pl.BlockSpec(memory_space=pltpu.HBM)
    vmem = pl.BlockSpec(memory_space=pltpu.VMEM)
    own = jax.ShapeDtypeStruct((N, N, DEPTH), jnp.float32)
    field = pltpu.VMEM((NXF, NYF, DEPTH), jnp.float32)
    fields = pl.pallas_call(
        exchange,
        out_shape=(field,) * 4,
        in_specs=[hbm] * 4,
        out_specs=(vmem,) * 4,
        scratch_shapes=[
            pltpu.VMEM((N + 2, 40, DEPTH), jnp.float32),
            pltpu.VMEM((N, N, DEPTH), jnp.float32),
            pltpu.VMEM((16, DEPTH), jnp.float32),
            pltpu.VMEM((3, 3 * N, N), jnp.int32),
            pltpu.VMEM((NYF, DEPTH), jnp.int32),
        ] + [pltpu.VMEM((2, N, DEPTH), jnp.float32)] * 8 + [
            pltpu.VMEM((4, 1, DEPTH), jnp.float32),
            pltpu.SemaphoreType.DMA((len(KEYS),)),
            pltpu.SemaphoreType.DMA((len(KEYS),)),
            pltpu.SemaphoreType.DMA((6,)),
        ],
        compiler_params=pltpu.CompilerParams(
            collective_id=0, has_side_effects=True, vmem_limit_bytes=24 << 20),
        name="exchange",
    )(*[pltpu.with_memory_space_constraint(a, pltpu.HBM)
        for a in (pressure, source, labels, region_table)])
    return pl.pallas_call(
        relax,
        out_shape=(own, own),
        in_specs=[vmem] * 4,
        out_specs=(hbm, hbm),
        scratch_shapes=[field] * 5 + [
            pltpu.VMEM((N, N, DEPTH), jnp.float32),
            pltpu.SemaphoreType.DMA((5,)),
        ],
        compiler_params=pltpu.CompilerParams(vmem_limit_bytes=24 << 20),
        name="relax",
    )(*fields)


def solution(mesh):
    placed = (P("space", "group", None), P("space", "group", None), P("space", "group"), P())
    return jax.shard_map(
        per_device,
        mesh=mesh,
        in_specs=placed,
        out_specs=(P("space", "group", None), P("space", "group", None)),
        check_vma=False,
    )
```

time: 29.5 us -> 28.2 us (0.956)
  the two profiles are of different devices: /device:TPU:6 before, /device:TPU:3 now
where the time goes in v5:
time: 28.2 us; the launch traced here: 28 us
  Pallas kernels  27.4 us (97%)
  between operations  0.64 us (2%)
    pallas_call x1, Pallas kernels, per_device(): pl.pallas_call(exchange, out_shape=(field,) * 4, in_specs=[hbm] * 4, out_...  23.4 us
    pallas_call x1, Pallas kernels, per_device(): pl.pallas_call(relax, out_shape=(own, own), in_specs=[vmem] * 4, out_spec...  3.99 us

profile of v5, /device:TPU:3, one launch (start us, length us, event | category | flops | bytes accessed | tf_op | source)
XLA Modules:
  0.0 28.0 jit_solution(2712390067892049338)
XLA Ops:
  0.6 23.4 %exchange.1 = (f32[66,72,128]{2,1,0:T(8,128)S(1)}, f32[66,72,128]{2,1,0:T(8,128)S(1)}, f32[66,72,128]{2,1,0:T(8,128)S(1)}, f32[66,72,128]{2,1,0:T(8,128)S(1)}) custom-call(f32[32,32,128]{2,1,0:T(8,128)} %p_hbm.1, f32[32,32,128]{2,1,0:T(8,128)} %src_hbm.1, s32[32,32]{1,0:T(8,128)} %lab_hbm.1, f32[16,128]{1,0:T(8,128)} %tab_hbm.1), custom_call_target="tpu_custom_call" | custom-call | tf_op jit(solution)/shard_map/exchange/pallas_call | solution.py:408
  24.0 4.0 %relax.1 = (f32[32,32,128]{2,1,0:T(8,128)}, f32[32,32,128]{2,1,0:T(8,128)}) custom-call(f32[66,72,128]{2,1,0:T(8,128)S(1)} %get-tuple-element.6.s_ref, f32[66,72,128]{2,1,0:T(8,128)S(1)} %get-tuple-element.7.w_ref, f32[66,72,128]{2,1,0:T(8,128)S(1)} %get-tuple-element.8.k_ref, f32[66,72,128]{2,1,0:T(8,128)S(1)} %get-tuple-element.9.rb), custom_call_target="tpu_custom_call" | custom-call | tf_op jit(solution)/shard_map/relax/pallas_call | solution.py:430

commit v6 on v5

--- a/solution.py
+++ b/solution.py
@@ -47,7 +47,7 @@
 
 
 def exchange(p_hbm, src_hbm, lab_hbm, tab_hbm, s_ref, w_ref, k_ref, rb,
-             pb, sb, tb, lb, lt, hx, hy, ax, ay, bx, by, rx, cy, cc,
+             pb, sb, tb, lbl, pk, lpk, lt, hx, hy, ax, ay, bx, by, rx, cy, cc,
              send, recv, local):
     groups = lax.axis_size("group")
     spaces = lax.axis_size("space")
@@ -77,7 +77,7 @@
                                     local.at[4 + h]) for h, (a, n) in enumerate(halves)]
     load_s = [pltpu.make_async_copy(src_hbm.at[pl.ds(a, n)], sb.at[pl.ds(a, n)],
                                     local.at[h]) for h, (a, n) in enumerate(halves)]
-    load_l = pltpu.make_async_copy(lab_hbm, lb.at[1, pl.ds(N, N), :], local.at[2])
+    load_l = pltpu.make_async_copy(lab_hbm, lbl, local.at[2])
     load_t = pltpu.make_async_copy(tab_hbm, tb, local.at[3])
     load_l.start()
     load_t.start()
@@ -99,7 +99,7 @@
         @pl.when(jnp.logical_not(there(d)))
         def _():
             dx, dy = d
-            lb[1 + dy, pl.ds(N * (1 + dx), N), :] = jnp.full((N, N), -1, jnp.int32)
+            lpk[1 + dy, 1 + dx] = jnp.full((8, DEPTH), -1, jnp.int32)
 
     for d in SIDES:
         @pl.when(jnp.logical_not(there(d)))
@@ -125,9 +125,7 @@
         ex, ey = int(dx > 0), int(dy > 0)
         last = N - 1
         if kind == 0:
-            r0, rows = (15, 17) if dx > 0 else (0, 17) if dx < 0 else (0, N)
-            ends = [(lab_hbm.at[pl.ds(r0, rows), :],
-                     lb.at[1 - dy, pl.ds(N * (1 - dx) + r0, rows), :])]
+            ends = [(pk, lpk.at[1 - dy, 1 - dx])]
         elif kind == 1:
             ends = [(p_hbm.at[last * ex], hx.at[1 - ex]) if dx
                     else (p_hbm.at[:, last * ey, :], hy.at[1 - ey])]
@@ -230,8 +228,15 @@
     own_x = list(range(XO, XO + N))
     load_l.wait()
     none = jnp.full((N, N), -1, jnp.int32)
+    mine = lbl[...]
+    pk[...] = jnp.concatenate([mine[8 * g:8 * g + 8] for g in range(4)], axis=1)
+
+    def block(dy, dx):
+        tile = lpk[dy, dx]
+        return jnp.concatenate([tile[:, N * g:N * g + N] for g in range(4)], axis=0)
+
     lt[...] = jnp.full((NYF, DEPTH), -1, jnp.int32)
-    lt[pl.ds(20, N), :] = tags(jnp.concatenate([none, lb[1, pl.ds(N, N), :], none], axis=0))
+    lt[pl.ds(20, N), :] = tags(jnp.concatenate([none, mine, none], axis=0))
 
     def vertical(weight, value):
         return weight * pltpu.roll(value, DEPTH - 1, 1) + pltpu.roll(weight * value, 1, 1)
@@ -271,15 +276,15 @@
 
         if h == 0:
             pl.semaphore_wait(barrier, count)
+            start([0], ORDER)
             start([1], SIDES)
-            start([0], DIRS)
         start([2 + h], ORDER)
 
     def outward(s, sn, p, pn):
         return (s + sn) * (p - pn) - s * p
 
     arrive([0, 1], XSIDES)
-    lt[pl.ds(20, N), :] = tags(lb[1])
+    lt[pl.ds(20, N), :] = tags(jnp.concatenate([block(1, 0), mine, block(1, 2)], axis=0))
     coefficients([XO - 1, XO + N], 16, 40)
     for e, (f, g) in enumerate(((XO, XO - 1), (XO + N - 1, XO + N))):
         s, sn = s_ref[f, own, :], s_ref[g, own, :]
@@ -291,8 +296,8 @@
     start([4], YSIDES)
 
     arrive([0, 1], YSIDES)
-    lt[pl.ds(0, 20), :] = tags(jnp.concatenate([none, lb[0, pl.ds(N, N), :], none], axis=0))[12:]
-    lt[pl.ds(52, 20), :] = tags(jnp.concatenate([none, lb[2, pl.ds(N, N), :], none], axis=0))[:20]
+    lt[pl.ds(0, 20), :] = tags(jnp.concatenate([none, block(0, 1), none], axis=0))[12:]
+    lt[pl.ds(52, 20), :] = tags(jnp.concatenate([none, block(2, 1), none], axis=0))[:20]
     coefficients(own_x, 16, 8)
     coefficients(own_x, 48, 8)
     rows = pl.ds(XO, N)
@@ -311,8 +316,8 @@
     start([6], CORNERS)
 
     arrive([0], CORNERS)
-    lt[pl.ds(0, 20), :] = tags(lb[0])[12:]
-    lt[pl.ds(52, 20), :] = tags(lb[2])[:20]
+    lt[pl.ds(0, 20), :] = tags(jnp.concatenate([block(0, n) for n in range(3)], axis=0))[12:]
+    lt[pl.ds(52, 20), :] = tags(jnp.concatenate([block(2, n) for n in range(3)], axis=0))[:20]
     for part in (range(0, XO - 1), range(XO + N + 1, NXF)):
         coefficients(list(part), 0, NYF)
     coefficients([XO - 1, XO + N], 0, 24)
@@ -414,7 +419,9 @@
             pltpu.VMEM((N + 2, 40, DEPTH), jnp.float32),
             pltpu.VMEM((N, N, DEPTH), jnp.float32),
             pltpu.VMEM((16, DEPTH), jnp.float32),
-            pltpu.VMEM((3, 3 * N, N), jnp.int32),
+            pltpu.VMEM((N, N), jnp.int32),
+            pltpu.VMEM((8, DEPTH), jnp.int32),
+            pltpu.VMEM((3, 3, 8, DEPTH), jnp.int32),
             pltpu.VMEM((NYF, DEPTH), jnp.int32),
         ] + [pltpu.VMEM((2, N, DEPTH), jnp.float32)] * 8 + [
             pltpu.VMEM((4, 1, DEPTH), jnp.float32),

time: 28.2 us -> 27.5 us (0.975)
  the two profiles are of different devices: /device:TPU:3 before, /device:TPU:6 now
where the time goes in v6:
time: 27.5 us; the launch traced here: 27.4 us
  Pallas kernels  26.7 us (97%)
  between operations  0.64 us (2%)
    pallas_call x1, Pallas kernels, per_device(): pl.pallas_call(exchange, out_shape=(field,) * 4, in_specs=[hbm] * 4, out_...  22.8 us
    pallas_call x1, Pallas kernels, per_device(): pl.pallas_call(relax, out_shape=(own, own), in_specs=[vmem] * 4, out_spec...  3.99 us

profile of v6, /device:TPU:6, one launch (start us, length us, event | category | flops | bytes accessed | tf_op | source)
XLA Modules:
  0.0 27.4 jit_solution(16582355630489520264)
XLA Ops:
  0.6 22.8 %exchange.1 = (f32[66,72,128]{2,1,0:T(8,128)S(1)}, f32[66,72,128]{2,1,0:T(8,128)S(1)}, f32[66,72,128]{2,1,0:T(8,128)S(1)}, f32[66,72,128]{2,1,0:T(8,128)S(1)}) custom-call(f32[32,32,128]{2,1,0:T(8,128)} %p_hbm.1, f32[32,32,128]{2,1,0:T(8,128)} %src_hbm.1, s32[32,32]{1,0:T(8,128)} %lab_hbm.1, f32[16,128]{1,0:T(8,128)} %tab_hbm.1), custom_call_target="tpu_custom_call" | custom-call | tf_op jit(solution)/shard_map/exchange/pallas_call | solution.py:413
  23.4 4.0 %relax.1 = (f32[32,32,128]{2,1,0:T(8,128)}, f32[32,32,128]{2,1,0:T(8,128)}) custom-call(f32[66,72,128]{2,1,0:T(8,128)S(1)} %get-tuple-element.6.s_ref, f32[66,72,128]{2,1,0:T(8,128)S(1)} %get-tuple-element.7.w_ref, f32[66,72,128]{2,1,0:T(8,128)S(1)} %get-tuple-element.8.k_ref, f32[66,72,128]{2,1,0:T(8,128)S(1)} %get-tuple-element.9.rb), custom_call_target="tpu_custom_call" | custom-call | tf_op jit(solution)/shard_map/relax/pallas_call | solution.py:437

commit v7 on v6

--- a/solution.py
+++ b/solution.py
@@ -11,7 +11,7 @@
 XO, YO = 17, 20
 NXF, NYF = 66, 72
 DIRS = [(dx, dy) for dx in (-1, 0, 1) for dy in (-1, 0, 1) if (dx, dy) != (0, 0)]
-ORDER = [(0, -1), (0, 1), (-1, -1), (-1, 1), (1, -1), (1, 1), (-1, 0), (1, 0)]
+ORDER = [(0, -1), (0, 1), (-1, 0), (1, 0), (-1, -1), (-1, 1), (1, -1), (1, 1)]
 DIRS_X, DIRS_Y = [(-1, 0), (1, 0)], [(0, -1), (0, 1)]
 DIRS_XY = [(-1, -1), (-1, 1), (1, -1), (1, 1)]
 SIDES = DIRS_X + DIRS_Y
@@ -37,7 +37,7 @@
 XSIDES, YSIDES, CORNERS = DIRS_X, DIRS_Y, DIRS_XY
 KINDS = {0: DIRS, 1: SIDES, 2: DIRS, 3: DIRS, 4: YSIDES, 5: XSIDES, 6: CORNERS}
 KEYS = [(kind, d, n) for kind, dirs in KINDS.items() for d in dirs
-        for n in range(len(pieces(d, kind - 2)) if kind in (2, 3) else (1, 1, 0, 0, 2, 2, 3)[kind])]
+        for n in range(len(pieces(d, kind - 2)) if kind in (2, 3) else (1, 1, 0, 0, 2, 2, 2)[kind])]
 
 
 def columns(reach, x):
@@ -47,7 +47,7 @@
 
 
 def exchange(p_hbm, src_hbm, lab_hbm, tab_hbm, s_ref, w_ref, k_ref, rb,
-             pb, sb, tb, lbl, pk, lpk, lt, hx, hy, ax, ay, bx, by, rx, cy, cc,
+             pb, sb, tb, lbl, pk, lpk, lt, hx, hy, ax, ay, bx, by, rx, cy, rc,
              send, recv, local):
     groups = lax.axis_size("group")
     spaces = lax.axis_size("space")
@@ -147,11 +147,10 @@
             ends = [(cy.at[e, pl.ds(x, 14), :],
                      rb.at[pl.ds(XO + x - N * dx, 14), YO + last * e, :]) for e in (0, 1)]
         else:
-            x, y = (N - 13 if ex else 1), (N - 13 if ey else 1)
+            x, y = (N - 13 if ex else 1), (N - 13) * ey
             fx, fy = XO + last * ex - N * dx, YO + last * ey - N * dy
-            ends = [(rx.at[ex, pl.ds(y, 12), :], rb.at[fx, pl.ds(YO + y - N * dy, 12), :]),
-                    (cy.at[ey, pl.ds(x, 12), :], rb.at[pl.ds(XO + x - N * dx, 12), fy, :]),
-                    (cc.at[2 * ex + ey], rb.at[fx, pl.ds(fy, 1), :])]
+            ends = [(rc.at[ex, pl.ds(y, 13), :], rb.at[fx, pl.ds(YO + y - N * dy, 13), :]),
+                    (cy.at[ey, pl.ds(x, 12), :], rb.at[pl.ds(XO + x - N * dx, 12), fy, :])]
         return [pltpu.make_async_remote_copy(
             src_ref=src, dst_ref=dst, send_sem=send.at[KEYS.index((kind, d, n))],
             recv_sem=recv.at[KEYS.index((kind, d, n))], device_id=device(d), device_id_type=MESH)
@@ -309,9 +308,10 @@
         by[e] = outward(sn, s, pn, p)
         cy[e] = rb[rows, f, :] - delta
     for ex in (0, 1):
+        rc[ex] = rx[ex]
         for ey in (0, 1):
-            cc[2 * ex + ey] = (rx[ex, pl.ds((N - 1) * ey, 1), :]
-                               - ay[ey, pl.ds((N - 1) * ex, 1), :])
+            at = pl.ds((N - 1) * ey, 1)
+            rc[ex, at, :] = rx[ex, at, :] - ay[ey, pl.ds((N - 1) * ex, 1), :]
     start([5], XSIDES)
     start([6], CORNERS)
 
@@ -424,7 +424,7 @@
             pltpu.VMEM((3, 3, 8, DEPTH), jnp.int32),
             pltpu.VMEM((NYF, DEPTH), jnp.int32),
         ] + [pltpu.VMEM((2, N, DEPTH), jnp.float32)] * 8 + [
-            pltpu.VMEM((4, 1, DEPTH), jnp.float32),
+            pltpu.VMEM((2, N, DEPTH), jnp.float32),
             pltpu.SemaphoreType.DMA((len(KEYS),)),
             pltpu.SemaphoreType.DMA((len(KEYS),)),
             pltpu.SemaphoreType.DMA((6,)),

time: 27.5 us -> 27.4 us (level)
  no operation moved by 1% of the time
where the time goes in v7:
time: 27.4 us; the launch traced here: 27.2 us
  Pallas kernels  26.6 us (97%)
  between operations  0.64 us (2%)
    pallas_call x1, Pallas kernels, per_device(): pl.pallas_call(exchange, out_shape=(field,) * 4, in_specs=[hbm] * 4, out_...  22.6 us
    pallas_call x1, Pallas kernels, per_device(): pl.pallas_call(relax, out_shape=(own, own), in_specs=[vmem] * 4, out_spec...  3.99 us

profile of v7, /device:TPU:6, one launch (start us, length us, event | category | flops | bytes accessed | tf_op | source)
XLA Modules:
  0.0 27.2 jit_solution(7533824641104846464)
XLA Ops:
  0.6 22.6 %exchange.1 = (f32[66,72,128]{2,1,0:T(8,128)S(1)}, f32[66,72,128]{2,1,0:T(8,128)S(1)}, f32[66,72,128]{2,1,0:T(8,128)S(1)}, f32[66,72,128]{2,1,0:T(8,128)S(1)}) custom-call(f32[32,32,128]{2,1,0:T(8,128)} %p_hbm.1, f32[32,32,128]{2,1,0:T(8,128)} %src_hbm.1, s32[32,32]{1,0:T(8,128)} %lab_hbm.1, f32[16,128]{1,0:T(8,128)} %tab_hbm.1), custom_call_target="tpu_custom_call" | custom-call | tf_op jit(solution)/shard_map/exchange/pallas_call | solution.py:413
  23.2 4.0 %relax.1 = (f32[32,32,128]{2,1,0:T(8,128)}, f32[32,32,128]{2,1,0:T(8,128)}) custom-call(f32[66,72,128]{2,1,0:T(8,128)S(1)} %get-tuple-element.6.s_ref, f32[66,72,128]{2,1,0:T(8,128)S(1)} %get-tuple-element.7.w_ref, f32[66,72,128]{2,1,0:T(8,128)S(1)} %get-tuple-element.8.k_ref, f32[66,72,128]{2,1,0:T(8,128)S(1)} %get-tuple-element.9.rb), custom_call_target="tpu_custom_call" | custom-call | tf_op jit(solution)/shard_map/relax/pallas_call | solution.py:437

commit v8 on v7

--- a/solution.py
+++ b/solution.py
@@ -23,7 +23,7 @@
         return [((1, 14), (1, N - 2))] if stage == (dx > 0) else []
     if dx == 0:
         return [((1, 15), (1, 14)) if stage == 0 else ((16, N - 2), (1, 14))]
-    return [((2, 6), (2, 12)), ((7, 12), (2, 6))] if stage == (dx > 0) else []
+    return [((2, 2), (2, 12)), ((3, 6), (2, 10)), ((7, 12), (2, 6))] if stage == (dx > 0) else []
 
 
 def span(step, lo, hi):

time: 27.4 us -> 27.4 us (level)
  no operation moved by 1% of the time
where the time goes in v8:
time: 27.4 us; the launch traced here: 27.3 us
  Pallas kernels  26.7 us (97%)
  between operations  0.64 us (2%)
    pallas_call x1, Pallas kernels, per_device(): pl.pallas_call(exchange, out_shape=(field,) * 4, in_specs=[hbm] * 4, out_...  22.7 us
    pallas_call x1, Pallas kernels, per_device(): pl.pallas_call(relax, out_shape=(own, own), in_specs=[vmem] * 4, out_spec...  3.99 us

profile of v8, /device:TPU:6, one launch (start us, length us, event | category | flops | bytes accessed | tf_op | source)
XLA Modules:
  0.0 27.3 jit_solution(15637773009899599207)
XLA Ops:
  0.6 22.7 %exchange.1 = (f32[66,72,128]{2,1,0:T(8,128)S(1)}, f32[66,72,128]{2,1,0:T(8,128)S(1)}, f32[66,72,128]{2,1,0:T(8,128)S(1)}, f32[66,72,128]{2,1,0:T(8,128)S(1)}) custom-call(f32[32,32,128]{2,1,0:T(8,128)} %p_hbm.1, f32[32,32,128]{2,1,0:T(8,128)} %src_hbm.1, s32[32,32]{1,0:T(8,128)} %lab_hbm.1, f32[16,128]{1,0:T(8,128)} %tab_hbm.1), custom_call_target="tpu_custom_call" | custom-call | tf_op jit(solution)/shard_map/exchange/pallas_call | solution.py:413
  23.3 4.0 %relax.1 = (f32[32,32,128]{2,1,0:T(8,128)}, f32[32,32,128]{2,1,0:T(8,128)}) custom-call(f32[66,72,128]{2,1,0:T(8,128)S(1)} %get-tuple-element.6.s_ref, f32[66,72,128]{2,1,0:T(8,128)S(1)} %get-tuple-element.7.w_ref, f32[66,72,128]{2,1,0:T(8,128)S(1)} %get-tuple-element.8.k_ref, f32[66,72,128]{2,1,0:T(8,128)S(1)} %get-tuple-element.9.rb), custom_call_target="tpu_custom_call" | custom-call | tf_op jit(solution)/shard_map/relax/pallas_call | solution.py:437
